TPU v7x, 32 devices: a whole 2x2x4 slice. The times are simulated.
32 devices in a mesh: groups: 2 (over y), view: 4 (over z), branch: 2 (over x), mp: 2 (over core).
Axes of the slice: x: 2, y: 2, z: 4, core: 2. Of those that a mesh axis runs over, the one named last changes fastest.
Arguments:
- tokens: bfloat16 [1024, 1024], P(('groups', 'view')), parts along dimension 0, may hold values from -6 to 6
- view_table: bfloat16 [4, 1024], replicated, may hold values from -6 to 6
- view_ids: int32 [8], P('groups'), parts along dimension 0, may hold values from 0 to 3, each once
- view_counts: int32 [8], P('groups'), parts along dimension 0, may hold values from 1 to 128, 384 in all
- norm_in_gain: float32 [1024], replicated, may hold values from 0.1 to 1.9
- in_weight: bfloat16 [1024, 4096], P(None, ('branch', 'mp')), may hold values from -0.1875 to 0.1875
- out_weight: bfloat16 [4096, 1024], P(('branch', 'mp')), may hold values from -0.09375 to 0.09375
- norm_attn_gain: float32 [1024], replicated, may hold values from 0.1 to 1.9
- qkv_weight: bfloat16 [1024, 3, 1024], P(None, None, ('branch', 'mp')), may hold values from -0.1875 to 0.1875
- head_gain: float32 [2, 64], replicated, may hold values from 0.6 to 4
- depth_weight: bfloat16 [1024, 256], P(('branch', 'mp')), may hold values from -0.1875 to 0.1875
- kernel_one: bfloat16 [3, 3, 256, 256], replicated, may hold values from -0.125 to 0.125
- bias_one: float32 [256], replicated, may hold values from -3 to 3
- kernel_two: bfloat16 [3, 3, 256, 256], replicated, may hold values from -0.125 to 0.125
- bias_two: float32 [256], replicated, may hold values from -3 to 3
- track_weight: bfloat16 [1024, 128], P(('branch', 'mp')), may hold values from -0.1875 to 0.1875
- track_ids: int32 [256], P('groups'), parts along dimension 0, may hold values from 0 to 511
Outputs:
- depth_out: bfloat16 [1024, 256], P(('groups', 'view', 'branch', 'mp')), parts along dimension 0
- track_out: float32 [256, 128], P(('groups', 'view', 'branch', 'mp')), parts along dimension 0
There are 2 independent parts, one for each index of `groups`. A program takes and returns all parts, laid end to end along the dimension named above; an argument that names none is the same for every part. Nothing has to cross between parts.
Inputs may be any that keep to these rules, and one draw needn't show every extreme that they name: `view_ids`: each slot names a different view. `view_counts`: some slot is full, with 128 valid tokens; the counts sum to 384.
All inputs are finite; a program needn't handle non-finite values.
Results may differ from a plain program's by a relative error of at most 0.023.
The roundings to bfloat16 on the way count: a program that leaves them out, or rounds other values in their place, can miss the bound.
Values may be sent and summed in bfloat16 or wider, within the bound.
No kernel may reach another device: no remote copies, remote signals or barrier semaphores. Data moves between devices by JAX's collectives and lax.ppermute only.
A program may use at most 64 MiB of HBM per device.

v0:
```python
import jax
import jax.numpy as jnp
from jax import lax
from jax.sharding import PartitionSpec as P

HD = 64
GW = 32


EPS_NORM = 1e-05
EPS_HEAD = 1e-06
NEG_FILL = -1e30
KEY_BLOCK = 1024


def with_halo(value, sides, width):
    for axis, dim in sides:
        size, length = (lax.axis_size(axis), value.shape[dim])
        up = [(i, (i + 1) % size) for i in range(size - 1)]
        down = [(j, i) for i, j in up]
        last = lax.slice_in_dim(value, length - width, length, axis=dim)
        first = lax.slice_in_dim(value, 0, width, axis=dim)
        before = lax.ppermute(last, axis, up)
        after = lax.ppermute(first, axis, down)
        value = jnp.concatenate([before, value, after], axis=dim)
    return value


def layer_norm(values, gain_vec):
    row_mean = jnp.mean(values, axis=-1, keepdims=True)
    centered = values - row_mean
    row_var = jnp.mean(centered * centered, axis=-1, keepdims=True)
    return centered * lax.rsqrt(row_var + EPS_NORM) * gain_vec


def head_norm(values, gain_vec):
    head_mean = jnp.mean(values, axis=-1, keepdims=True)
    centered = values - head_mean
    head_var = jnp.mean(centered * centered, axis=-1, keepdims=True)
    return centered * lax.rsqrt(head_var + EPS_HEAD) * gain_vec


def conv_rows(grid_field, kernel, bias_vec):
    extended = with_halo(grid_field, ((("branch", "mp"), 0),), GW)
    grid_height = grid_field.shape[0] // GW
    channels = grid_field.shape[1]
    shaped = extended.reshape(grid_height + 2, GW, channels)
    padded = jnp.pad(shaped, ((0, 0), (1, 1), (0, 0)))
    running_sum = jnp.zeros((grid_height * GW, kernel.shape[3]), jnp.float32)
    for row_off in range(3):
        for col_off in range(3):
            window = padded[row_off : row_off + grid_height, col_off : col_off + GW, :].reshape(
                -1, channels
            )
            running_sum = running_sum + jnp.dot(
                window, kernel[row_off, col_off], preferred_element_type=jnp.float32
            )
    return running_sum + bias_vec


def attend_piece(fold_state, piece_rows, first_row, query_heads, view_counts, tok_view, heads_dev):
    run_max, run_sum, run_acc = fold_state
    length = piece_rows.shape[0]
    head_width = heads_dev * HD
    score_scale = 1.0 / HD**0.5
    slot_range = jnp.arange(view_counts.shape[0], dtype=jnp.int32)
    for offset in range(0, length, KEY_BLOCK):
        block_size = min(KEY_BLOCK, length - offset)
        key_block = piece_rows[offset : offset + block_size]
        key_part = key_block[:, :head_width].reshape(block_size, heads_dev, HD)
        value_part = key_block[:, head_width:].reshape(block_size, heads_dev, HD)
        positions = first_row + offset + jnp.arange(block_size, dtype=jnp.int32)
        slot_view = positions // tok_view
        view_match = slot_view[:, None] == slot_range[None, :]
        view_limit = jnp.sum(jnp.where(view_match, view_counts[None, :], 0), axis=1)
        key_valid = positions % tok_view < view_limit
        scores = (
            jnp.einsum("qhd,khd->hqk", query_heads, key_part, preferred_element_type=jnp.float32)
            * score_scale
        )
        scores = jnp.where(key_valid[None, None, :], scores, NEG_FILL)
        new_max = jnp.maximum(run_max, jnp.max(scores, axis=2))
        weights = jnp.where(key_valid[None, None, :], jnp.exp(scores - new_max[:, :, None]), 0.0)
        rescale = jnp.exp(run_max - new_max)
        run_sum = run_sum * rescale + jnp.sum(weights, axis=2)
        run_acc = run_acc * rescale[:, :, None] + jnp.einsum(
            "hqk,khd->hqd",
            weights.astype(jnp.bfloat16),
            value_part,
            preferred_element_type=jnp.float32,
        )
        run_max = new_max
    return (run_max, run_sum, run_acc)


def select_rows(table_rows, wanted):
    row_total = table_rows.shape[0]
    inside = (wanted >= 0) & (wanted < row_total)
    picked = jnp.take(table_rows, jnp.clip(wanted, 0, row_total - 1), axis=0)
    return jnp.where(inside[:, None], picked, 0.0)


def local(
    tokens,
    view_table,
    view_ids,
    view_counts,
    norm_in_gain,
    in_weight,
    out_weight,
    norm_attn_gain,
    qkv_weight,
    head_gain,
    depth_weight,
    kernel_one,
    bias_one,
    kernel_two,
    bias_two,
    track_weight,
    track_ids,
):
    tok_view = tokens.shape[0]
    view_index = lax.axis_index("view")
    inner_index = lax.axis_index(("branch", "mp"))
    inner_count = lax.axis_size(("branch", "mp"))
    head_width = qkv_weight.shape[2]
    heads_dev = head_width // HD
    slot_match = jnp.arange(view_ids.shape[0], dtype=jnp.int32) == view_index
    my_view = jnp.sum(jnp.where(slot_match, view_ids, 0))
    my_count = jnp.sum(jnp.where(slot_match, view_counts, 0))
    table_pick = (jnp.arange(view_table.shape[0], dtype=jnp.int32) == my_view).astype(jnp.float32)
    view_embed = jnp.dot(
        table_pick, view_table.astype(jnp.float32), precision=lax.Precision.HIGHEST
    )
    residual_in = tokens.astype(jnp.float32) + view_embed[None, :]
    normed_in = layer_norm(residual_in, norm_in_gain).astype(jnp.bfloat16)
    hidden = jax.nn.gelu(
        jnp.dot(normed_in, in_weight, preferred_element_type=jnp.float32), approximate=True
    ).astype(jnp.bfloat16)
    share_rows = tok_view // inner_count
    row_block = hidden
    summed = lax.psum_scatter(
        jnp.dot(row_block, out_weight, preferred_element_type=jnp.float32),
        ("branch", "mp"),
        scatter_dimension=0,
        tiled=True,
    )
    own_residual = lax.dynamic_slice_in_dim(residual_in, inner_index * share_rows, share_rows, 0)
    mlp_out = (own_residual + summed).astype(jnp.bfloat16)
    normed_share = layer_norm(mlp_out.astype(jnp.float32), norm_attn_gain).astype(jnp.bfloat16)
    normed_attn = lax.all_gather(normed_share, ("branch", "mp"), axis=0, tiled=True)
    projected = jnp.dot(
        normed_attn,
        qkv_weight.reshape(qkv_weight.shape[0], 3 * head_width),
        preferred_element_type=jnp.float32,
    )
    query_heads = head_norm(
        projected[:, :head_width].reshape(tok_view, heads_dev, HD), head_gain[0]
    ).astype(jnp.bfloat16)
    key_heads = head_norm(
        projected[:, head_width : 2 * head_width].reshape(tok_view, heads_dev, HD), head_gain[1]
    ).astype(jnp.bfloat16)
    value_heads = projected[:, 2 * head_width :].astype(jnp.bfloat16)
    stacked = jnp.concatenate([key_heads.reshape(tok_view, head_width), value_heads], axis=1)
    fold_start = (
        jnp.full((heads_dev, tok_view), NEG_FILL, jnp.float32),
        jnp.zeros((heads_dev, tok_view), jnp.float32),
        jnp.zeros((heads_dev, tok_view, HD), jnp.float32),
    )
    run_max, run_sum, run_acc = attend_piece(
        fold_start,
        lax.all_gather(stacked, "view", axis=0, tiled=True),
        jnp.int32(0),
        query_heads,
        view_counts,
        tok_view,
        heads_dev,
    )
    attended = (
        (run_acc / run_sum[:, :, None])
        .astype(jnp.bfloat16)
        .transpose(1, 0, 2)
        .reshape(tok_view, head_width)
    )
    depth_rows = tok_view // inner_count
    row_pos = inner_index * depth_rows + jnp.arange(depth_rows, dtype=jnp.int32)
    row_valid = (row_pos < my_count).astype(jnp.float32)[:, None]
    row_block = attended
    depth_sum = lax.psum_scatter(
        jnp.dot(row_block, depth_weight, preferred_element_type=jnp.float32).astype(jnp.bfloat16),
        ("branch", "mp"),
        scatter_dimension=0,
        tiled=True,
    ).astype(jnp.float32)
    track_proj = jnp.dot(attended, track_weight, preferred_element_type=jnp.float32)
    wanted = track_ids - view_index * tok_view
    track_out = lax.psum_scatter(
        select_rows(track_proj, wanted), ("view", "branch", "mp"), scatter_dimension=0, tiled=True
    )
    features = (depth_sum * row_valid).astype(jnp.bfloat16)
    first_conv = jnp.maximum(conv_rows(features, kernel_one, bias_one), 0.0).astype(jnp.bfloat16)
    depth_out = conv_rows(first_conv, kernel_two, bias_two).astype(jnp.bfloat16)
    return (depth_out, track_out)


def solution(mesh):
    in_specs = (
        P(("groups", "view"), None),
        P(),
        P("groups"),
        P("groups"),
        P(),
        P(None, ("branch", "mp")),
        P(("branch", "mp"), None),
        P(),
        P(None, None, ("branch", "mp")),
        P(),
        P(("branch", "mp"), None),
        P(),
        P(),
        P(),
        P(),
        P(("branch", "mp"), None),
        P("groups"),
    )
    out_specs = (
        P(("groups", "view", "branch", "mp"), None),
        P(("groups", "view", "branch", "mp"), None),
    )
    return jax.shard_map(local, mesh=mesh, in_specs=in_specs, out_specs=out_specs, check_vma=False)
```

profile of v0, /device:TPU:0, one launch (start us, length us, event | category | flops | bytes accessed | tf_op | source)
XLA Modules:
  0.0 204.0 jit_solution(3850391703200718305)
XLA Ops:
  7.2 1.4 fusion.121
  8.7 1.5 fusion.120
  10.1 1.1 convert_add_fusion
  11.2 1.2 multiply_reduce_fusion
  12.4 3.4 %fusion.27 = f32[128,1024]{1,0:T(8,128)} fusion(bf16[1024,1024]{1,0:T(8,128)(2,1)S(1)} %copy-done, bf16[1024,1024]{1,0:T(8,128)(2,1)} %param.22, bf16[128,1024]{1,0:T(8,128)(2,1)} %param.17, f32[1024]{0:T(1024)} %param.21, f32[128]{0:T(128)S(1)} %add_rsqrt_fusion.3, f32[128]{0:T(128)S(1)} %broadcast_multiply_fusion.3, f32[1024]{0:T(1024)S(1)} %bitcast.176), kind=kOutput, calls=%fused_computation.49 | convolution fusion | flops 538836992 | bytes 4989952 | tf_op jit(solution)/shard_map/dot_general | solution.py:143
  15.8 0.0 reduce-scatter.5.cloned.1.call-start
  15.9 0.5 slice_bitcast_fusion.1
  16.4 2.6 %copy.38 = bf16[1024,3,256]{0,2,1:T(8,128)(2,1)} copy(bf16[1024,3,256]{2,0,1:T(8,128)(2,1)} %param.25) | data formatting | bytes 3145728 | tf_op args[8]
  19.1 0.1 mul.169
  19.2 0.6 dynamic-slice
  20.4 0.6 fusion.122
  21.0 1.2 compare_convert_fusion
  22.3 0.6 compare_and_fusion
  22.9 0.1 select_reduce_fusion
  23.0 17.4 %reduce-scatter.3.cloned.1.call-done = f32[32,1024]{1,0:T(8,128)} async-done(((f32[128,1024]{1,0:T(8,128)}), f32[32,1024]{1,0:T(8,128)}) %reduce-scatter.3.cloned.1.call-update) | async-done | bytes 131088 | tf_op jit(solution)/shard_map/reduce_scatter | solution.py:142
  40.4 1.0 convert_reduce_fusion
  41.4 0.2 fusion.42
  41.6 0.1 fusion.44
  41.7 5.8 %all_gather.6 = bf16[128,1024]{1,0:T(8,128)(2,1)S(1)} all-gather(bf16[32,1024]{1,0:T(8,128)(2,1)S(1)} %fusion.44), channel_id=1, replica_groups=mesh['groups'=2,'view'=4,'branch'=2,'mp'=2] {'branch','mp'}, dimensions={0}, use_global_device_ids=true | all-gather | bytes 327680 | tf_op jit(solution)/shard_map/all_gather | solution.py:151
  47.5 2.1 %fusion.145 = f32[128,768]{1,0:T(8,128)S(1)} fusion(bf16[128,1024]{1,0:T(8,128)(2,1)S(1)} %all_gather.6, bf16[1024,768]{0,1:T(8,128)(2,1)} %bitcast.155), kind=kOutput, calls=%fused_computation.208 | convolution fusion | flops 201326592 | bytes 2228224 | tf_op jit(solution)/shard_map/dot_general | solution.py:152
  49.6 0.1 copy.40
  49.8 0.1 copy.42
  49.9 0.1 copy.41
  50.1 0.1 copy.39
  50.3 16.1 %all_gather.7 = bf16[512,512]{1,0:T(8,128)(2,1)S(1)} all-gather(bf16[128,512]{1,0:T(8,128)(2,1)S(1)} %pad_maximum_fusion), channel_id=1, replica_groups=mesh['groups'=2,'view'=4,'branch'=2,'mp'=2] {'view'}, dimensions={0}, use_global_device_ids=true | all-gather | bytes 655360 | tf_op jit(solution)/shard_map/all_gather | solution.py:172
  66.3 0.7 fusion.142
  67.1 0.1 copy.43
  67.2 1.2 fusion.144
  68.4 0.3 fusion.11
  68.7 0.6 copy-done.2
  69.3 0.8 copy.44
  70.2 1.4 fusion.3
  71.6 0.8 convolution_convert_fusion
  72.4 0.0 all-reduce.5.cloned.1.call-start
  72.5 0.2 fusion.146
  72.7 0.7 gather_fusion
  73.3 19.3 %reduce-scatter.5.cloned.1.call-done = bf16[32,256]{1,0:T(8,128)(2,1)} async-done(((bf16[128,256]{1,0:T(8,128)(2,1)}), bf16[32,256]{1,0:T(8,128)(2,1)}) %reduce-scatter.5.cloned.1.call-update) | async-done | bytes 16400 | tf_op jit(solution)/shard_map/reduce_scatter | solution.py:189
  92.7 0.8 multiply_convert_fusion.9
  93.5 1.3 collective-permute-start
  94.7 1.3 collective-permute-start.1
  96.1 0.7 select_select_fusion
  96.8 1.4 collective-permute-done.1
  98.2 0.1 fusion.65
  98.4 0.2 fusion.56
  98.5 0.2 convolution_add_fusion.13
  98.7 0.2 convolution_add_fusion.12
  98.8 0.2 convolution_add_fusion.11
  99.0 0.2 convolution_add_fusion.10
  99.1 0.2 convolution_add_fusion.9
  99.3 0.2 convolution_add_fusion.8
  99.4 0.2 fusion.9
  99.6 4.4 %collective-permute-start.2 = (bf16[32,256]{1,0:T(8,128)(2,1)S(1)}, bf16[32,256]{1,0:T(8,128)(2,1)S(1)}, u32[]{:S(2)}, u32[]{:S(2)}) collective-permute-start(bf16[32,256]{1,0:T(8,128)(2,1)S(1)} %fusion.9), channel_id=1, source_target_pairs={{0,1},{1,2},{2,3},{4,5},{5,6},{6,7},{8,9},{9,10},{10,11},{12,13},{... | collective-permute-start | bytes 49160 | tf_op jit(solution)/shard_map/ppermute | solution.py:23
  104.0 1.3 collective-permute-start.3
  105.3 80.8 %all-reduce.5.cloned.1.call-done = f32[128,128]{1,0:T(8,128)} async-done(((f32[128,128]{1,0:T(8,128)}), f32[128,128]{1,0:T(8,128)}) %all-reduce.5.cloned.1.call-update) | async-done | bytes 65552
  186.1 1.3 constant_dynamic-slice_fusion
  187.4 1.0 fusion.54
  188.5 1.1 fusion.45
  189.5 1.1 convolution_add_fusion.6
  190.6 1.1 convolution_add_fusion.5
  191.6 1.1 convolution_add_fusion.4
  192.7 1.1 convolution_add_fusion.3
  193.7 1.1 convolution_add_fusion.2
  194.8 1.1 convolution_add_fusion.1
  195.8 1.7 fusion.10
  (62 shorter events, 0.5 us)
Async XLA Ops:
  7.2 5.2 %copy-start = (bf16[1024,1024]{1,0:T(8,128)(2,1)S(1)}, bf16[1024,1024]{1,0:T(8,128)(2,1)}, u32[]{:S(2)}) copy-start(bf16[1024,1024]{1,0:T(8,128)(2,1)} %param.23) | copy-start | bytes 6291460
  7.2 33.2 %reduce-scatter.3.cloned.1.call-start = ((), (), s32[]{:S(2)}) async-start(), calls=%async_computation.2 | async-start | bytes 655360 | tf_op jit(solution)/shard_map/reduce_scatter | solution.py:142
  12.4 3.5 %copy-start.10 = (f32[2,64]{1,0:T(2,128)S(1)}, f32[2,64]{1,0:T(2,128)}, u32[]{:S(2)}) copy-start(f32[2,64]{1,0:T(2,128)} %param.26) | copy-start | bytes 1540
  15.8 76.8 %reduce-scatter.5.cloned.1.call-start = ((), (), s32[]{:S(2)}) async-start(), calls=%async_computation.3 | async-start | bytes 81920 | tf_op jit(solution)/shard_map/reduce_scatter | solution.py:189
  16.4 2.7 %copy-start.14 = (u32[32]{0:T(128)S(1)}, u32[32]{0:T(128)}, u32[]{:S(2)}) copy-start(u32[32]{0:T(128)} %constant.109) | copy-start | bytes 388
  16.4 4.0 %copy-start.13 = (s32[4]{0:T(128)S(1)}, s32[4]{0:T(128)}, u32[]{:S(2)}) copy-start(s32[4]{0:T(128)} %param.20) | copy-start | bytes 52
  16.4 5.9 %copy-start.12 = (s32[128]{0:T(128)S(1)}, s32[128]{0:T(128)}, u32[]{:S(2)}) copy-start(s32[128]{0:T(128)} %param.33) | copy-start | bytes 1540
  16.4 25.2 %copy-start.5 = (f32[1024]{0:T(1024)S(1)}, f32[1024]{0:T(1024)}, u32[]{:S(2)}) copy-start(f32[1024]{0:T(1024)} %param.24) | copy-start | bytes 12292
  68.4 1.0 copy-start.2
  70.2 1.4 copy-start.3
  70.2 2.3 %copy-start.4 = (bf16[256,128]{1,0:T(8,128)(2,1)S(1)}, bf16[256,128]{1,0:T(8,128)(2,1)}, u32[]{:S(2)}) copy-start(bf16[256,128]{1,0:T(8,128)(2,1)} %param.32) | copy-start | bytes 196612
  70.2 22.5 %copy-start.11 = (f32[32]{0:T(128)S(1)}, f32[32]{0:T(128)}, u32[]{:S(2)}) copy-start(f32[32]{0:T(128)} %compare_convert_fusion) | copy-start | bytes 388
  70.2 25.9 %copy-start.6 = (pred[128]{0:T(512)(128)(4,1)S(1)}, pred[128]{0:T(512)(128)(4,1)}, u32[]{:S(2)}) copy-start(pred[128]{0:T(512)(128)(4,1)} %get-tuple-element.2) | copy-start | bytes 388
  70.2 25.9 %copy-start.7 = (pred[128]{0:T(512)(128)(4,1)S(1)}, pred[128]{0:T(512)(128)(4,1)}, u32[]{:S(2)}) copy-start(pred[128]{0:T(512)(128)(4,1)} %get-tuple-element.16) | copy-start | bytes 388
  71.6 26.7 %copy-start.1 = (bf16[3,3,256,256]{3,2,1,0:T(8,128)(2,1)S(1)}, bf16[3,3,256,256]{3,2,1,0:T(8,128)(2,1)}, u32[]{:S(2)}) copy-start(bf16[3,3,256,256]{3,2,1,0:T(8,128)(2,1)} %param.28) | copy-start | bytes 3538948
  72.4 113.7 %all-reduce.5.cloned.1.call-start = ((), (), s32[]{:S(2)}) async-start(), calls=%async_computation.4 | async-start | bytes 131072
  73.3 26.1 %copy-start.8 = (f32[256]{0:T(256)S(1)}, f32[256]{0:T(256)}, u32[]{:S(2)}) copy-start(f32[256]{0:T(256)} %param.29) | copy-start | bytes 3076
  93.5 3.4 %collective-permute-start = (bf16[32,256]{1,0:T(8,128)(2,1)S(1)}, bf16[32,256]{1,0:T(8,128)(2,1)S(1)}, u32[]{:S(2)}, u32[]{:S(2)}) collective-permute-start(bf16[32,256]{1,0:T(8,128)(2,1)S(1)} %multiply_convert_fusion.9), channel_id=1, source_target_pairs={{0,1},{1,2},{2,3},{4,5},{5,6},{6,7},{8,9},{9,10},{10,11},{12,13},{... | collective-permute-start | bytes 49160 | tf_op jit(solution)/shard_map/ppermute | solution.py:23
  94.7 3.5 %collective-permute-start.1 = (bf16[32,256]{1,0:T(8,128)(2,1)S(1)}, bf16[32,256]{1,0:T(8,128)(2,1)S(1)}, u32[]{:S(2)}, u32[]{:S(2)}) collective-permute-start(bf16[32,256]{1,0:T(8,128)(2,1)S(1)} %multiply_convert_fusion.9), channel_id=1, source_target_pairs={{1,0},{2,1},{3,2},{5,4},{6,5},{7,6},{9,8},{10,9},{11,10},{13,12},{... | collective-permute-start | bytes 49160 | tf_op jit(solution)/shard_map/ppermute | solution.py:24
  99.3 96.6 %copy-start.9 = (f32[256]{0:T(256)S(1)}, f32[256]{0:T(256)}, u32[]{:S(2)}) copy-start(f32[256]{0:T(256)} %param.31) | copy-start | bytes 3076
  99.6 87.8 %collective-permute-start.2 = (bf16[32,256]{1,0:T(8,128)(2,1)S(1)}, bf16[32,256]{1,0:T(8,128)(2,1)S(1)}, u32[]{:S(2)}, u32[]{:S(2)}) collective-permute-start(bf16[32,256]{1,0:T(8,128)(2,1)S(1)} %fusion.9), channel_id=1, source_target_pairs={{0,1},{1,2},{2,3},{4,5},{5,6},{6,7},{8,9},{9,10},{10,11},{12,13},{... | collective-permute-start | bytes 49160 | tf_op jit(solution)/shard_map/ppermute | solution.py:23
  104.0 83.4 %collective-permute-start.3 = (bf16[32,256]{1,0:T(8,128)(2,1)S(1)}, bf16[32,256]{1,0:T(8,128)(2,1)S(1)}, u32[]{:S(2)}, u32[]{:S(2)}) collective-permute-start(bf16[32,256]{1,0:T(8,128)(2,1)S(1)} %fusion.9), channel_id=1, source_target_pairs={{1,0},{2,1},{3,2},{5,4},{6,5},{7,6},{9,8},{10,9},{11,10},{13,12},{... | collective-permute-start | bytes 49160 | tf_op jit(solution)/shard_map/ppermute | solution.py:24
Sparse Core Ops, SparseCore 0:
  16.0 24.3 reduce-scatter.2
  72.5 20.0 reduce-scatter.4
  96.9 89.1 all-reduce.4
where the time goes:
time: 206 us; the launch traced here: 204 us
  waiting for transfers between devices  119 us (58%)
  matrix products  21.9 us (11%)
  blocking collectives  21.9 us (11%)
  between operations  14.7 us (7%)
  other arithmetic  9.59 us (5%)
  local copies, waits for them, and re-layouts  8.52 us (4%)
  starting transfers between devices  8.37 us (4%)
    unnamed x4, waiting for transfers between devices  80.9 us
    reduce_scatter x1, waiting for transfers between devices, local(): lax.psum_scatter(jnp.dot(row_block, depth_weight, preferred_element_type=...  19.3 us
    reduce_scatter x1, waiting for transfers between devices, local(): lax.psum_scatter(jnp.dot(row_block, out_weight, preferred_element_type=jn...  17.4 us
    all_gather x1, blocking collectives, local(): lax.all_gather(stacked, 'view', axis=0, tiled=True)  16.1 us
    dot_general x18, matrix products, conv_rows(): jnp.dot(window, kernel[row_off, col_off], preferred_element_type=jnp.floa...  11.5 us
    all_gather x1, blocking collectives, local(): lax.all_gather(normed_share, ('branch', 'mp'), axis=0, tiled=True)  5.78 us
    ppermute x2, starting transfers between devices, with_halo(): before = lax.ppermute(last, axis, up)  5.66 us
    unnamed x33, local copies, waits for them, and re-layouts  5.17 us
  transfers between devices with their start and end apart: 7, of which 4 were waited for; matrix products, arithmetic and copies ran while one was open for 5% of the time, Pallas kernels for 0%

commit v1 on v0

--- a/solution.py
+++ b/solution.py
@@ -203,6 +203,184 @@
     return (depth_out, track_out)
 
 
+def xor_pairs(size, step):
+    return [(i, i ^ step) for i in range(size)]
+
+
+def peers(value, axis, size):
+    return [lax.ppermute(value, axis, xor_pairs(size, k)) for k in range(1, size)]
+
+
+def shift_cols(rows, col_off):
+    height = rows.shape[0] // GW
+    shaped = jnp.pad(rows.reshape(height, GW, -1), ((0, 0), (1, 1), (0, 0)))
+    return shaped[:, col_off : col_off + GW, :].reshape(rows.shape)
+
+
+def conv_valid(rows, kernel, bias_vec):
+    out_rows = rows.shape[0] - 2 * GW
+    total = bias_vec[None, :] + jnp.zeros((out_rows, kernel.shape[3]), jnp.float32)
+    for col_off in range(3):
+        shifted = shift_cols(rows, col_off)
+        for row_off in range(3):
+            total = total + jnp.dot(
+                shifted[row_off * GW : row_off * GW + out_rows],
+                kernel[row_off, col_off],
+                preferred_element_type=jnp.float32,
+            )
+    return total
+
+
+def local_fast(
+    tokens,
+    view_table,
+    view_ids,
+    view_counts,
+    norm_in_gain,
+    in_weight,
+    out_weight,
+    norm_attn_gain,
+    qkv_weight,
+    head_gain,
+    depth_weight,
+    kernel_one,
+    bias_one,
+    kernel_two,
+    bias_two,
+    track_weight,
+    track_ids,
+):
+    tok_view = tokens.shape[0]
+    views = lax.axis_size("view")
+    branches, cores = lax.axis_size("branch"), lax.axis_size("mp")
+    inner_axes = ("branch", "mp")
+    inner_count = branches * cores
+    view_index = lax.axis_index("view")
+    inner_index = lax.axis_index(inner_axes)
+    head_width = qkv_weight.shape[2]
+    heads_dev = head_width // HD
+    share = tok_view // inner_count
+    my_view = view_ids[view_index]
+    view_embed = view_table[my_view].astype(jnp.float32)
+    residual_in = tokens.astype(jnp.float32) + view_embed[None, :]
+    normed_in = layer_norm(residual_in, norm_in_gain).astype(jnp.bfloat16)
+    hidden = jax.nn.gelu(
+        jnp.dot(normed_in, in_weight, preferred_element_type=jnp.float32), approximate=True
+    ).astype(jnp.bfloat16)
+    part = jnp.dot(hidden, out_weight, preferred_element_type=jnp.float32)
+    for axis, size in (("mp", cores), ("branch", branches)):
+        sent = part.astype(jnp.bfloat16)
+        part = sent.astype(jnp.float32)
+        for got in peers(sent, axis, size):
+            part = part + got.astype(jnp.float32)
+    mlp_out = (residual_in + part).astype(jnp.bfloat16)
+    normed_attn = layer_norm(mlp_out.astype(jnp.float32), norm_attn_gain).astype(jnp.bfloat16)
+    projected = jnp.dot(
+        normed_attn,
+        qkv_weight.reshape(qkv_weight.shape[0], 3 * head_width),
+        preferred_element_type=jnp.float32,
+    )
+    queries = (
+        head_norm(projected[:, :head_width].reshape(tok_view, heads_dev, HD), head_gain[0])
+        .astype(jnp.bfloat16)
+        .reshape(tok_view, head_width)
+    )
+    keys = (
+        head_norm(
+            projected[:, head_width : 2 * head_width].reshape(tok_view, heads_dev, HD), head_gain[1]
+        )
+        .astype(jnp.bfloat16)
+        .reshape(tok_view, head_width)
+    )
+    values = projected[:, 2 * head_width :].astype(jnp.bfloat16)
+    stacked = jnp.concatenate([keys, values], axis=1)
+    asked = track_ids.shape[0] // views
+    wanted = track_ids - view_index * tok_view
+    pick = (wanted[:, None] == jnp.arange(tok_view, dtype=jnp.int32)[None, :]).astype(jnp.bfloat16)
+    picked = jnp.dot(pick, queries, preferred_element_type=jnp.float32).astype(jnp.bfloat16)
+    half = asked // 2
+
+    def message(k):
+        mine = lax.dynamic_slice_in_dim(picked, (view_index ^ k) * asked, asked, 0)
+        mine = jnp.concatenate([mine[:half], mine[half:]], axis=1)
+        return jnp.concatenate([stacked, mine], axis=0)
+
+    blocks = [message(0)] + [
+        lax.ppermute(message(k), "view", xor_pairs(views, k)) for k in range(1, views)
+    ]
+    asked_rows = blocks[0][tok_view:].astype(jnp.float32)
+    for block in blocks[1:]:
+        asked_rows = asked_rows + block[tok_view:].astype(jnp.float32)
+    asked_rows = asked_rows.astype(jnp.bfloat16)
+    asked_rows = jnp.concatenate([asked_rows[:, :head_width], asked_rows[:, head_width:]], axis=0)
+    all_queries = jnp.concatenate([queries, asked_rows], axis=0).reshape(-1, heads_dev, HD)
+    score_scale = 1.0 / HD**0.5
+    scores = []
+    for k, block in enumerate(blocks):
+        part_keys = block[:tok_view, :head_width].reshape(tok_view, heads_dev, HD)
+        valid = jnp.arange(tok_view, dtype=jnp.int32) < view_counts[view_index ^ k]
+        score = (
+            jnp.einsum("qhd,khd->hqk", all_queries, part_keys, preferred_element_type=jnp.float32)
+            * score_scale
+        )
+        scores.append(jnp.where(valid[None, None, :], score, NEG_FILL))
+    scores = jnp.concatenate(scores, axis=2)
+    row_max = jnp.max(scores, axis=2, keepdims=True)
+    weights = jnp.exp(scores - row_max)
+    row_sum = jnp.sum(weights, axis=2, keepdims=True)
+    all_values = jnp.concatenate([block[:tok_view, head_width:] for block in blocks], axis=0)
+    mixed = jnp.einsum(
+        "hqk,khd->hqd",
+        weights.astype(jnp.bfloat16),
+        all_values.reshape(-1, heads_dev, HD),
+        preferred_element_type=jnp.float32,
+    )
+    attended = (mixed / row_sum).astype(jnp.bfloat16).transpose(1, 0, 2).reshape(-1, head_width)
+    depth_part = jnp.dot(
+        attended[:tok_view], depth_weight, preferred_element_type=jnp.float32
+    ).astype(jnp.bfloat16)
+    track_part = jnp.dot(
+        attended[tok_view:], track_weight, preferred_element_type=jnp.float32
+    ).astype(jnp.bfloat16)
+    own = asked // inner_count
+    depth_sum = depth_part.astype(jnp.float32)
+    track_sum = lax.dynamic_slice_in_dim(track_part, inner_index * own, own, 0).astype(jnp.float32)
+    for k in range(1, inner_count):
+        rows = lax.dynamic_slice_in_dim(track_part, (inner_index ^ k) * own, own, 0)
+        rows = jnp.pad(rows, ((0, 0), (0, depth_part.shape[1] - rows.shape[1])))
+        got = lax.ppermute(
+            jnp.concatenate([depth_part, rows], axis=0), inner_axes, xor_pairs(inner_count, k)
+        ).astype(jnp.float32)
+        depth_sum = depth_sum + got[:tok_view]
+        track_sum = track_sum + got[tok_view:, : track_part.shape[1]]
+    my_count = view_counts[view_index]
+    row_valid = (jnp.arange(tok_view, dtype=jnp.int32) < my_count).astype(jnp.float32)[:, None]
+    features = (depth_sum * row_valid).astype(jnp.bfloat16)
+    near = share + 4 * GW
+    padded = jnp.pad(features, ((2 * GW, 2 * GW), (0, 0)))
+    window = lax.dynamic_slice_in_dim(padded, inner_index * share, near, 0)
+    first = jnp.maximum(conv_valid(window, kernel_one, bias_one), 0.0)
+    place = inner_index * share - GW + jnp.arange(near - 2 * GW, dtype=jnp.int32)
+    inside = (place >= 0) & (place < tok_view)
+    first = jnp.where(inside[:, None], first, 0.0).astype(jnp.bfloat16)
+    depth_out = conv_valid(first, kernel_two, bias_two).astype(jnp.bfloat16)
+    return (depth_out, track_sum)
+
+
+def power_of_two(size):
+    return size & (size - 1) == 0
+
+
+def pick_path(*args):
+    tok_view, head_width = args[0].shape[0], args[8].shape[2]
+    sizes = [lax.axis_size(axis) for axis in ("view", "branch", "mp")]
+    inner_count = sizes[1] * sizes[2]
+    share = tok_view // inner_count
+    fits = all(power_of_two(size) for size in sizes) and share % GW == 0
+    fits = fits and head_width % 128 == 0 and (args[16].shape[0] // sizes[0]) % inner_count == 0
+    return local_fast(*args) if fits else local(*args)
+
+
 def solution(mesh):
     in_specs = (
         P(("groups", "view"), None),
@@ -227,4 +405,4 @@
         P(("groups", "view", "branch", "mp"), None),
         P(("groups", "view", "branch", "mp"), None),
     )
-    return jax.shard_map(local, mesh=mesh, in_specs=in_specs, out_specs=out_specs, check_vma=False)
+    return jax.shard_map(pick_path, mesh=mesh, in_specs=in_specs, out_specs=out_specs, check_vma=False)

time: 206 us -> 58.1 us (0.28)
  waiting for transfers between devices: 119 us -> 15.7 us
  blocking collectives: 21.9 us -> 0 us
  between operations: 14.7 us -> 3.15 us
  matrix products: 21.9 us -> 11.7 us
    unnamed x4 -> x0, waiting for transfers between devices: 80.9 us -> none
    reduce_scatter x2 -> x0, waiting for transfers between devices: 36.7 us -> none  [the longest x1 19.3 us: local(): lax.psum_scatter(jnp.dot(row_block, depth_weight, preferred_element_type=...]
    all_gather x2 -> x0, blocking collectives: 21.9 us -> none  [the longest x1 16.1 us: local(): lax.all_gather(stacked, 'view', axis=0, tiled=True)]
    ppermute x4 -> x8, waiting for transfers between devices: 1.41 us -> 15.7 us  [the longest x3 9.02 us: local_fast(): lax.ppermute(message(k), 'view', xor_pairs(views, k))]
    dot_general x25 -> x28, matrix products: 21.9 us -> 11.7 us  [the longest x18 3.45 us: conv_valid(): jnp.dot(shifted[row_off * GW:row_off * GW + out_rows], kernel[row_off, co...]
    lt x1 -> x4, other arithmetic: 0.01 us -> 4.62 us  [local_fast(): valid = jnp.arange(tok_view, dtype=jnp.int32) < view_counts[view_index ^ k]]
    dynamic_slice x0 -> x4, local copies, waits for them, and re-layouts: none -> 2.13 us  [the longest x1 1.39 us: local_fast(): my_view = view_ids[view_index]]
    unnamed x33 -> x31, local copies, waits for them, and re-layouts: 5.17 us -> 3.35 us
  transfers between devices with their start and end apart: 7 -> 8, of which waited for: 4 -> 5; matrix products, arithmetic and copies ran while one was open for 5% -> 15% of each run, Pallas kernels for 0% -> 0%
where the time goes in v1:
time: 58.1 us; the launch traced here: 57.7 us
  waiting for transfers between devices  15.7 us (27%)
  matrix products  11.7 us (20%)
  other arithmetic  10.3 us (18%)
  starting transfers between devices  9.56 us (16%)
  local copies, waits for them, and re-layouts  7.24 us (12%)
  between operations  3.15 us (5%)
    ppermute x3, waiting for transfers between devices, local_fast(): lax.ppermute(message(k), 'view', xor_pairs(views, k))  9.02 us
    lt x4, other arithmetic, local_fast(): valid = jnp.arange(tok_view, dtype=jnp.int32) < view_counts[view_index ^ k]  4.62 us
    ppermute x3, starting transfers between devices, local_fast(): lax.ppermute(message(k), 'view', xor_pairs(views, k))  4.48 us
    ppermute x3, waiting for transfers between devices, local_fast(): lax.ppermute(jnp.concatenate([depth_part, rows], axis=0), inner_axes, xor...  3.9 us
    dot_general x18, matrix products, conv_valid(): jnp.dot(shifted[row_off * GW:row_off * GW + out_rows], kernel[row_off, co...  3.45 us
    unnamed x31, local copies, waits for them, and re-layouts  3.35 us
    ppermute x2, starting transfers between devices, peers(): lax.ppermute(value, axis, xor_pairs(size, k))  3.16 us
    ppermute x2, waiting for transfers between devices, peers(): lax.ppermute(value, axis, xor_pairs(size, k))  2.81 us
  transfers between devices with their start and end apart: 8, of which 5 were waited for; matrix products, arithmetic and copies ran while one was open for 15% of the time, Pallas kernels for 0%

profile of v1, /device:TPU:0, one launch (start us, length us, event | category | flops | bytes accessed | tf_op | source)
XLA Modules:
  0.0 57.7 jit_solution(11687733014803880132)
XLA Ops:
  0.7 1.4 %dynamic_slice.47 = s32[1]{0:T(128)} dynamic-slice(s32[4]{0:T(128)} %param.19, s32[]{:T(128)S(6)} %select_n.61), dynamic_slice_sizes={1} | dynamic-slice | bytes 12 | tf_op jit(solution)/shard_map/dynamic_slice | solution.py:263
  4.0 0.7 %fusion.115 = f32[1,1024]{1,0:T(1,128)S(1)} fusion(bf16[4,1024]{1,0:T(4,128)(2,1)} %param.18, s32[]{:T(128)S(6)} %select_n.62), kind=kLoop, calls=%fused_computation.189 | loop fusion | flops 1024 | bytes 6148 | tf_op jit(solution)/shard_map/add | solution.py:265
  4.7 1.1 %fusion.28 = f32[128]{0:T(128)S(1)} fusion(bf16[128,1024]{1,0:T(8,128)(2,1)} %param.17, f32[1024]{0:T(1024)S(1)} %bitcast.167), kind=kLoop, calls=%fused_computation.63 | loop fusion | flops 393088 | bytes 266752 | tf_op jit(solution)/shard_map/reduce_sum | solution.py:30
  5.8 1.2 %multiply_reduce_fusion = f32[128]{0:T(128)S(1)} fusion(bf16[128,1024]{1,0:T(8,128)(2,1)} %param.17, f32[128]{0:T(128)S(1)} %broadcast_multiply_fusion.3, f32[1024]{0:T(1024)S(1)} %bitcast.168), kind=kLoop, calls=%fused_computation.60 | loop fusion | flops 655232 | bytes 267264 | tf_op jit(solution)/shard_map/reduce_sum | solution.py:32
  7.0 2.6 %convolution_convert_fusion = bf16[128,1024]{1,0:T(8,128)(2,1)S(1)} fusion(bf16[1024,1024]{1,0:T(8,128)(2,1)S(1)} %copy-done, bf16[1024,1024]{1,0:T(8,128)(2,1)} %param.22, bf16[128,1024]{1,0:T(8,128)(2,1)} %param.17, f32[1024]{0:T(1024)} %param.21, f32[128]{0:T(128)S(1)} %add_rsqrt_fusion.3, f32[128]{0:T(128)S(1)} %broadcast_multiply_fusion.3, ...), kind=kOutput, calls=%fused_computation.2 | convolution fusion | flops 538968064 | bytes 4727808 | tf_op jit(solution)/shard_map/dot_general | solution.py:270
  9.6 0.6 collective-permute-start
  10.1 0.7 %fusion.136 = (s32[1]{0:T(128)}, s32[1]{0:T(128)}, s32[1]{0:T(128)}, s32[1]{0:T(128)}) fusion(s32[4]{0:T(128)S(1)} %copy-done.6, s32[]{:T(128)S(6)} %select_n.61, s32[]{:T(128)S(6)} %select_n.68, s32[]{:T(128)S(6)} %select_n.72, s32[]{:T(128)S(6)} %select_n.70), kind=kLoop, calls=%fused_computation.230 | loop fusion | bytes 48 | tf_op jit(solution)/shard_map/dynamic_slice | solution.py:321
  10.8 1.2 %iota_compare_fusion.6 = pred[128]{0:T(512)(128)(4,1)} fusion(s32[]{:T(128)} %bitcast), kind=kLoop, calls=%fused_computation.206 | loop fusion | flops 128 | bytes 132 | tf_op jit(solution)/shard_map/lt | solution.py:321
  12.0 0.6 %fusion.130 = f32[128]{0:T(128)S(1)} fusion(s32[]{:T(128)} %bitcast), kind=kLoop, calls=%fused_computation.224 | loop fusion | flops 256 | bytes 516 | tf_op jit(solution)/shard_map/convert_element_type | solution.py:357
  12.7 2.6 %collective-permute-start.1 = (bf16[128,1024]{1,0:T(8,128)(2,1)S(1)}, bf16[128,1024]{1,0:T(8,128)(2,1)S(1)}, u32[]{:S(2)}, u32[]{:S(2)}) collective-permute-start(bf16[128,1024]{1,0:T(8,128)(2,1)S(1)} %add_convert_fusion.1), channel_id=1, source_target_pairs={{0,2},{2,0},{1,3},{3,1},{4,6},{6,4},{5,7},{7,5},{8,10},{10,8},{9,1... | collective-permute-start | bytes 786440 | tf_op jit(solution)/shard_map/ppermute | solution.py:211
  15.3 1.2 %iota_compare_fusion.5 = pred[128]{0:T(512)(128)(4,1)} fusion(s32[]{:T(128)} %bitcast.15), kind=kLoop, calls=%fused_computation.201 | loop fusion | flops 128 | bytes 132 | tf_op jit(solution)/shard_map/lt | solution.py:321
  16.6 2.7 %copy.31 = bf16[1024,3,256]{0,2,1:T(8,128)(2,1)} copy(bf16[1024,3,256]{2,0,1:T(8,128)(2,1)} %param.25) | data formatting | bytes 3145728 | tf_op args[8]
  19.5 2.8 %collective-permute-done.1 = bf16[128,1024]{1,0:T(8,128)(2,1)S(1)} collective-permute-done((bf16[128,1024]{1,0:T(8,128)(2,1)S(1)}, bf16[128,1024]{1,0:T(8,128)(2,1)S(1)}, u32[]{:S(2)}, u32[]{:S(2)}) %collective-permute-start.1) | collective-permute-done | bytes 262176 | tf_op jit(solution)/shard_map/ppermute | solution.py:211
  22.3 0.2 convert_reduce_fusion
  22.5 0.2 fusion.16
  22.7 2.1 %fusion.30 = f32[128,768]{1,0:T(8,128)S(1)} fusion(bf16[1024,768]{0,1:T(8,128)(2,1)} %bitcast.146, bf16[128,1024]{1,0:T(8,128)(2,1)S(1)} %get-tuple-element.3, f32[1024]{0:T(1024)S(1)} %copy-done.7, f32[128]{0:T(128)S(1)} %add_rsqrt_fusion.2, f32[128]{0:T(128)S(1)} %broadcast_multiply_fusion.2), kind=kOutput, calls=%fused_computation.65 | convolution fusion | flops 201981952 | bytes 2233344 | tf_op jit(solution)/shard_map/dot_general | solution.py:278
  25.1 0.1 copy.34
  25.8 0.2 convolution_convert_fusion.1
  26.1 1.9 %collective-permute-start.2 = (bf16[144,512]{1,0:T(8,128)(2,1)S(1)}, bf16[144,512]{1,0:T(8,128)(2,1)S(1)}, u32[]{:S(2)}, u32[]{:S(2)}) collective-permute-start(bf16[144,512]{1,0:T(8,128)(2,1)S(1)} %get-tuple-element.14), channel_id=1, source_target_pairs={{0,4},{4,0},{8,12},{12,8},{1,5},{5,1},{9,13},{13,9},{2,6},{6,2},{1... | collective-permute-start | bytes 442376 | tf_op jit(solution)/shard_map/ppermute | solution.py:309
  28.0 2.6 %collective-permute-start.3 = (bf16[144,512]{1,0:T(8,128)(2,1)S(1)}, bf16[144,512]{1,0:T(8,128)(2,1)S(1)}, u32[]{:S(2)}, u32[]{:S(2)}) collective-permute-start(bf16[144,512]{1,0:T(8,128)(2,1)S(1)} %get-tuple-element.15), channel_id=1, source_target_pairs={{0,8},{4,12},{8,0},{12,4},{1,9},{5,13},{9,1},{13,5},{2,10},{6,14},... | collective-permute-start | bytes 442376 | tf_op jit(solution)/shard_map/ppermute | solution.py:309
  30.5 1.1 %iota_compare_fusion.4 = pred[128]{0:T(512)(128)(4,1)} fusion(s32[]{:T(128)} %bitcast.17), kind=kLoop, calls=%fused_computation.200 | loop fusion | flops 128 | bytes 132 | tf_op jit(solution)/shard_map/lt | solution.py:321
  31.6 1.1 %iota_compare_fusion.3 = pred[128]{0:T(512)(128)(4,1)} fusion(s32[]{:T(128)} %bitcast.19), kind=kLoop, calls=%fused_computation.199 | loop fusion | flops 128 | bytes 132 | tf_op jit(solution)/shard_map/lt | solution.py:321
  32.7 0.1 copy.35
  32.9 0.8 %collective-permute-done.2 = bf16[144,512]{1,0:T(8,128)(2,1)S(1)} collective-permute-done((bf16[144,512]{1,0:T(8,128)(2,1)S(1)}, bf16[144,512]{1,0:T(8,128)(2,1)S(1)}, u32[]{:S(2)}, u32[]{:S(2)}) %collective-permute-start.2) | collective-permute-done | bytes 147488 | tf_op jit(solution)/shard_map/ppermute | solution.py:309
  33.6 8.2 %collective-permute-done.3 = bf16[144,512]{1,0:T(8,128)(2,1)S(1)} collective-permute-done((bf16[144,512]{1,0:T(8,128)(2,1)S(1)}, bf16[144,512]{1,0:T(8,128)(2,1)S(1)}, u32[]{:S(2)}, u32[]{:S(2)}) %collective-permute-start.3) | collective-permute-done | bytes 147488 | tf_op jit(solution)/shard_map/ppermute | solution.py:309
  41.9 0.1 copy.45
  42.0 0.1 copy.46
  42.2 0.1 copy.41
  42.3 0.1 copy.42
  42.5 0.1 copy.43
  42.6 0.1 copy.44
  42.8 1.1 %fusion.139 = (f32[4,160]{1,0:T(4,128)S(1)}, f32[4,160,128]{2,1,0:T(8,128)S(1)}) fusion(f32[128,256]{0,1:T(8,128)S(1)} %copy.36, f32[64]{0:T(128)S(1)} %get-tuple-element.39, f32[128,4]{0,1:T(4,128)S(1)} %add_rsqrt_fusion, f32[128,4]{0,1:T(4,128)S(1)} %broadcast_multiply_fusion, bf16[16,4,64]{0,2,1:T(8,128)(2,1)S(1)} %bitcast.175, ...), kind=kOutput, calls=%fused_computation.233 | convolution fusion | flops 11107712 | bytes 547712 | tf_op jit(solution)/shard_map/qhd,khd->hqk/dot_general | solution.py:323
  43.9 0.5 fusion.140
  44.4 0.5 fusion.138
  44.8 0.5 fusion.137
  45.3 0.5 fusion.14
  45.9 0.5 fusion.6
  46.4 0.4 copy-done.4
  46.8 0.2 convolution_convert_fusion.2
  47.0 0.2 convolution_convert_fusion.3
  47.3 1.5 %collective-permute-start.6 = (bf16[136,256]{1,0:T(8,128)(2,1)S(1)}, bf16[136,256]{1,0:T(8,128)(2,1)S(1)}, u32[]{:S(2)}, u32[]{:S(2)}) collective-permute-start(bf16[136,256]{1,0:T(8,128)(2,1)S(1)} %get-tuple-element.24), channel_id=1, source_target_pairs={{0,2},{1,3},{2,0},{3,1},{4,6},{5,7},{6,4},{7,5},{8,10},{9,11},{10,... | collective-permute-start | bytes 208904 | tf_op jit(solution)/shard_map/ppermute | solution.py:351
  48.8 0.3 collective-permute-start.7
  49.1 2.8 %collective-permute-done.6 = bf16[136,256]{1,0:T(8,128)(2,1)S(1)} collective-permute-done((bf16[136,256]{1,0:T(8,128)(2,1)S(1)}, bf16[136,256]{1,0:T(8,128)(2,1)S(1)}, u32[]{:S(2)}, u32[]{:S(2)}) %collective-permute-start.6) | collective-permute-done | bytes 69664 | tf_op jit(solution)/shard_map/ppermute | solution.py:351
  51.9 1.1 %collective-permute-done.7 = bf16[136,256]{1,0:T(8,128)(2,1)S(1)} collective-permute-done((bf16[136,256]{1,0:T(8,128)(2,1)S(1)}, bf16[136,256]{1,0:T(8,128)(2,1)S(1)}, u32[]{:S(2)}, u32[]{:S(2)}) %collective-permute-start.7) | collective-permute-done | bytes 69664 | tf_op jit(solution)/shard_map/ppermute | solution.py:351
  53.1 0.6 %slice_add_fusion.3 = f32[8,128]{1,0:T(8,128)} fusion(f32[136,256]{1,0:T(8,128)S(1)} %convert_element_type.154, f32[136,256]{1,0:T(8,128)S(1)} %convert_element_type.153, f32[136,256]{1,0:T(8,128)S(1)} %convert_element_type.152, bf16[32,128]{1,0:T(8,128)(2,1)S(1)} %convolution_convert_fusion.3, s32[]{:T(128)S(6)} %select_n.79), kind=kLoop, calls=%fused_computation.190 | loop fusion | flops 4096 | bytes 18436 | tf_op jit(solution)/shard_map/add | solution.py:355
  53.9 0.2 convolution_add_fusion.8
  54.1 0.2 convolution_add_fusion.7
  54.2 0.2 convolution_add_fusion.6
  54.4 0.2 convolution_add_fusion.5
  54.6 0.2 convolution_add_fusion.4
  54.8 0.2 convolution_add_fusion.3
  55.0 0.2 convolution_add_fusion.2
  55.1 0.2 convolution_add_fusion.1
  55.3 0.2 fusion.9
  55.5 0.2 copy-done.3
  55.7 0.1 convolution_add_fusion.17
  55.8 0.1 convolution_add_fusion.16
  56.0 0.2 convolution_add_fusion.15
  56.1 0.2 convolution_add_fusion.14
  56.3 0.2 convolution_add_fusion.13
  56.4 0.2 convolution_add_fusion.12
  56.6 0.2 convolution_add_fusion.11
  56.7 0.2 convolution_add_fusion.10
  56.9 0.8 %fusion.10 = bf16[32,256]{1,0:T(8,128)(2,1)} fusion(f32[32,256]{1,0:T(8,128)S(1)} %convolution_add_fusion.10, bf16[3,3,256,256]{3,2,1,0:T(8,128)(2,1)S(1)} %copy-done.3, bf16[3,32,256]{2,1,0:T(8,128)(2,1)S(1)} %bitcast.152), kind=kOutput, calls=%fused_computation.37 | convolution fusion | flops 4210688 | bytes 229376 | tf_op jit(solution)/shard_map/dot_general | solution.py:226
  (84 shorter events, 1.6 us)
Async XLA Ops:
  0.6 6.3 %copy-start = (bf16[1024,1024]{1,0:T(8,128)(2,1)S(1)}, bf16[1024,1024]{1,0:T(8,128)(2,1)}, u32[]{:S(2)}) copy-start(bf16[1024,1024]{1,0:T(8,128)(2,1)} %param.23) | copy-start | bytes 6291460
  6.9 3.2 %copy-start.6 = (s32[4]{0:T(128)S(1)}, s32[4]{0:T(128)}, u32[]{:S(2)}) copy-start(s32[4]{0:T(128)} %param.20) | copy-start | bytes 52
  7.0 5.7 %copy-start.10 = (f32[2,64]{1,0:T(2,128)S(1)}, f32[2,64]{1,0:T(2,128)}, u32[]{:S(2)}) copy-start(f32[2,64]{1,0:T(2,128)} %param.26) | copy-start | bytes 1540
  9.6 3.1 %collective-permute-start = (bf16[128,1024]{1,0:T(8,128)(2,1)S(1)}, bf16[128,1024]{1,0:T(8,128)(2,1)S(1)}, u32[]{:S(2)}, u32[]{:S(2)}) collective-permute-start(bf16[128,1024]{1,0:T(8,128)(2,1)S(1)} %convolution_convert_fusion), channel_id=1, source_target_pairs={{0,1},{1,0},{2,3},{3,2},{4,5},{5,4},{6,7},{7,6},{8,9},{9,8},{10,11... | collective-permute-start | bytes 786440 | tf_op jit(solution)/shard_map/ppermute | solution.py:211
  12.7 9.5 %collective-permute-start.1 = (bf16[128,1024]{1,0:T(8,128)(2,1)S(1)}, bf16[128,1024]{1,0:T(8,128)(2,1)S(1)}, u32[]{:S(2)}, u32[]{:S(2)}) collective-permute-start(bf16[128,1024]{1,0:T(8,128)(2,1)S(1)} %add_convert_fusion.1), channel_id=1, source_target_pairs={{0,2},{2,0},{1,3},{3,1},{4,6},{6,4},{5,7},{7,5},{8,10},{10,8},{9,1... | collective-permute-start | bytes 786440 | tf_op jit(solution)/shard_map/ppermute | solution.py:211
  16.6 2.9 %copy-start.11 = (s32[128]{0:T(128)S(1)}, s32[128]{0:T(128)}, u32[]{:S(2)}) copy-start(s32[128]{0:T(128)} %param.33) | copy-start | bytes 1540
  16.6 5.7 %copy-start.1 = (bf16[128,1024]{1,0:T(8,128)(2,1)S(1)}, bf16[128,1024]{1,0:T(8,128)(2,1)}, u32[]{:S(2)}) copy-start(bf16[128,1024]{1,0:T(8,128)(2,1)} %param.17) | copy-start | bytes 786436
  19.3 3.4 %copy-start.7 = (f32[1024]{0:T(1024)S(1)}, f32[1024]{0:T(1024)}, u32[]{:S(2)}) copy-start(f32[1024]{0:T(1024)} %param.24) | copy-start | bytes 12292
  26.1 7.6 %collective-permute-start.2 = (bf16[144,512]{1,0:T(8,128)(2,1)S(1)}, bf16[144,512]{1,0:T(8,128)(2,1)S(1)}, u32[]{:S(2)}, u32[]{:S(2)}) collective-permute-start(bf16[144,512]{1,0:T(8,128)(2,1)S(1)} %get-tuple-element.14), channel_id=1, source_target_pairs={{0,4},{4,0},{8,12},{12,8},{1,5},{5,1},{9,13},{13,9},{2,6},{6,2},{1... | collective-permute-start | bytes 442376 | tf_op jit(solution)/shard_map/ppermute | solution.py:309
  28.0 13.9 %collective-permute-start.3 = (bf16[144,512]{1,0:T(8,128)(2,1)S(1)}, bf16[144,512]{1,0:T(8,128)(2,1)S(1)}, u32[]{:S(2)}, u32[]{:S(2)}) collective-permute-start(bf16[144,512]{1,0:T(8,128)(2,1)S(1)} %get-tuple-element.15), channel_id=1, source_target_pairs={{0,8},{4,12},{8,0},{12,4},{1,9},{5,13},{9,1},{13,5},{2,10},{6,14},... | collective-permute-start | bytes 442376 | tf_op jit(solution)/shard_map/ppermute | solution.py:309
  30.5 11.4 %collective-permute-start.4 = (bf16[144,512]{1,0:T(8,128)(2,1)S(1)}, bf16[144,512]{1,0:T(8,128)(2,1)S(1)}, u32[]{:S(2)}, u32[]{:S(2)}) collective-permute-start(bf16[144,512]{1,0:T(8,128)(2,1)S(1)} %get-tuple-element.16), channel_id=1, source_target_pairs={{0,12},{4,8},{8,4},{12,0},{1,13},{5,9},{9,5},{13,1},{2,14},{6,10},... | collective-permute-start | bytes 442376 | tf_op jit(solution)/shard_map/ppermute | solution.py:309
  42.3 1.6 %copy-start.12 = (pred[128]{0:T(512)(128)(4,1)S(1)}, pred[128]{0:T(512)(128)(4,1)}, u32[]{:S(2)}) copy-start(pred[128]{0:T(512)(128)(4,1)} %iota_compare_fusion.5) | copy-start | bytes 388
  42.6 1.8 %copy-start.13 = (pred[128]{0:T(512)(128)(4,1)S(1)}, pred[128]{0:T(512)(128)(4,1)}, u32[]{:S(2)}) copy-start(pred[128]{0:T(512)(128)(4,1)} %iota_compare_fusion.4) | copy-start | bytes 388
  42.8 2.1 %copy-start.14 = (pred[128]{0:T(512)(128)(4,1)S(1)}, pred[128]{0:T(512)(128)(4,1)}, u32[]{:S(2)}) copy-start(pred[128]{0:T(512)(128)(4,1)} %iota_compare_fusion.3) | copy-start | bytes 388
  45.8 0.9 %copy-start.4 = (bf16[256,256]{1,0:T(8,128)(2,1)S(1)}, bf16[256,256]{1,0:T(8,128)(2,1)}, u32[]{:S(2)}) copy-start(bf16[256,256]{1,0:T(8,128)(2,1)} %param.27) | copy-start | bytes 393220
  45.9 1.1 %copy-start.5 = (bf16[256,128]{1,0:T(8,128)(2,1)S(1)}, bf16[256,128]{1,0:T(8,128)(2,1)}, u32[]{:S(2)}) copy-start(bf16[256,128]{1,0:T(8,128)(2,1)} %param.32) | copy-start | bytes 196612
  46.8 7.1 %copy-start.2 = (bf16[3,3,256,256]{3,2,1,0:T(8,128)(2,1)S(1)}, bf16[3,3,256,256]{3,2,1,0:T(8,128)(2,1)}, u32[]{:S(2)}) copy-start(bf16[3,3,256,256]{3,2,1,0:T(8,128)(2,1)} %param.28) | copy-start | bytes 3538948
  46.8 7.2 %copy-start.8 = (f32[256]{0:T(256)S(1)}, f32[256]{0:T(256)}, u32[]{:S(2)}) copy-start(f32[256]{0:T(256)} %param.29) | copy-start | bytes 3076
  47.2 1.9 %collective-permute-start.5 = (bf16[136,256]{1,0:T(8,128)(2,1)S(1)}, bf16[136,256]{1,0:T(8,128)(2,1)S(1)}, u32[]{:S(2)}, u32[]{:S(2)}) collective-permute-start(bf16[136,256]{1,0:T(8,128)(2,1)S(1)} %get-tuple-element.23), channel_id=1, source_target_pairs={{0,1},{1,0},{2,3},{3,2},{4,5},{5,4},{6,7},{7,6},{8,9},{9,8},{10,11... | collective-permute-start | bytes 208904 | tf_op jit(solution)/shard_map/ppermute | solution.py:351
  47.3 4.6 %collective-permute-start.6 = (bf16[136,256]{1,0:T(8,128)(2,1)S(1)}, bf16[136,256]{1,0:T(8,128)(2,1)S(1)}, u32[]{:S(2)}, u32[]{:S(2)}) collective-permute-start(bf16[136,256]{1,0:T(8,128)(2,1)S(1)} %get-tuple-element.24), channel_id=1, source_target_pairs={{0,2},{1,3},{2,0},{3,1},{4,6},{5,7},{6,4},{7,5},{8,10},{9,11},{10,... | collective-permute-start | bytes 208904 | tf_op jit(solution)/shard_map/ppermute | solution.py:351
  48.8 4.3 %collective-permute-start.7 = (bf16[136,256]{1,0:T(8,128)(2,1)S(1)}, bf16[136,256]{1,0:T(8,128)(2,1)S(1)}, u32[]{:S(2)}, u32[]{:S(2)}) collective-permute-start(bf16[136,256]{1,0:T(8,128)(2,1)S(1)} %get-tuple-element.25), channel_id=1, source_target_pairs={{0,3},{1,2},{2,1},{3,0},{4,7},{5,6},{6,5},{7,4},{8,11},{9,10},{10,... | collective-permute-start | bytes 208904 | tf_op jit(solution)/shard_map/ppermute | solution.py:351
  54.4 1.3 %copy-start.3 = (bf16[3,3,256,256]{3,2,1,0:T(8,128)(2,1)S(1)}, bf16[3,3,256,256]{3,2,1,0:T(8,128)(2,1)}, u32[]{:S(2)}) copy-start(bf16[3,3,256,256]{3,2,1,0:T(8,128)(2,1)} %param.30) | copy-start | bytes 3538948
  54.4 1.3 %copy-start.9 = (f32[256]{0:T(256)S(1)}, f32[256]{0:T(256)}, u32[]{:S(2)}) copy-start(f32[256]{0:T(256)} %param.31) | copy-start | bytes 3076

commit v2 on v0

--- a/solution.py
+++ b/solution.py
@@ -1,6 +1,10 @@
+import functools
+
 import jax
 import jax.numpy as jnp
 from jax import lax
+from jax.experimental import pallas as pl
+from jax.experimental.pallas import tpu as pltpu
 from jax.sharding import PartitionSpec as P
 
 HD = 64
@@ -203,6 +207,333 @@
     return (depth_out, track_out)
 
 
+VMEM = pl.BlockSpec(memory_space=pltpu.VMEM)
+SMEM = pl.BlockSpec(memory_space=pltpu.SMEM)
+COLUMNS = 256
+VMEM_GRANT = 16 << 20
+OPEN_GRANT = 1 << 20
+
+
+def dot(left, right):
+    return jnp.dot(left, right, preferred_element_type=jnp.float32)
+
+
+def run_kernel(body, out_shape, in_specs, scratch=(), grant=VMEM_GRANT, cost=None):
+    return pl.pallas_call(
+        body,
+        out_shape=out_shape,
+        in_specs=in_specs,
+        out_specs=jax.tree.map(lambda _: VMEM, out_shape),
+        scratch_shapes=list(scratch),
+        compiler_params=pltpu.CompilerParams(vmem_limit_bytes=grant),
+        cost_estimate=cost,
+    )
+
+
+def xor_pairs(size, step):
+    return [(i, i ^ step) for i in range(size)]
+
+
+def peers(value, axis, size):
+    return [lax.ppermute(value, axis, xor_pairs(size, k)) for k in range(1, size)]
+
+
+def column_blocks(width):
+    return [slice(low, min(low + COLUMNS, width)) for low in range(0, width, COLUMNS)]
+
+
+def open_kernel(out_ref):
+    out_ref[...] = jnp.zeros(out_ref.shape, out_ref.dtype)
+
+
+def mlp_kernel(
+    ids_ref, table_ref, tokens_ref, gain_ref, in_ref, out_ref, open_ref, part_ref, embed_ref, hidden_ref
+):
+    my_view = ids_ref[lax.axis_index("view")]
+    row = lax.broadcasted_iota(jnp.int32, table_ref.shape, 0)
+    table = table_ref[...].astype(jnp.float32)
+    embed_ref[...] = jnp.sum(jnp.where(row == my_view, table, 0.0), axis=0, keepdims=True)
+    residual = tokens_ref[...].astype(jnp.float32) + embed_ref[...]
+    normed = layer_norm(residual, gain_ref[...]).astype(jnp.bfloat16)
+    for cols in column_blocks(in_ref.shape[1]):
+        hidden_ref[:, cols] = jax.nn.gelu(dot(normed, in_ref[:, cols]), approximate=True).astype(
+            jnp.bfloat16
+        )
+    hidden = hidden_ref[...]
+    for cols in column_blocks(out_ref.shape[1]):
+        part_ref[:, cols] = dot(hidden, out_ref[:, cols]).astype(jnp.bfloat16)
+
+
+def split_dot(values, mixer):
+    high = values.astype(jnp.bfloat16)
+    rest = values - high.astype(jnp.float32)
+    middle = rest.astype(jnp.bfloat16)
+    low = (rest - middle.astype(jnp.float32)).astype(jnp.bfloat16)
+    return dot(high, mixer) + dot(middle, mixer) + dot(low, mixer)
+
+
+def norm_heads(values, gain):
+    width = values.shape[1]
+    row = lax.broadcasted_iota(jnp.int32, (width, width), 0) // HD
+    col = lax.broadcasted_iota(jnp.int32, (width, width), 1) // HD
+    mixer = jnp.where(row == col, 1.0 / HD, 0.0).astype(jnp.bfloat16)
+    centered = values - split_dot(values, mixer)
+    spread = split_dot(centered * centered, mixer)
+    return (centered * lax.rsqrt(spread + EPS_HEAD) * gain).astype(jnp.bfloat16)
+
+
+def project_kernel(
+    embed_ref,
+    tokens_ref,
+    *refs,
+    sums,
+    views,
+):
+    sum_refs, refs = refs[:sums], refs[sums:]
+    gain_ref, qkv_ref, head_gain_ref, track_ref = refs[:4]
+    query_ref, message_refs, picked_ref = refs[4], refs[5 : 5 + views], refs[5 + views]
+    tok_view, width = query_ref.shape
+    total = tokens_ref[...].astype(jnp.float32) + embed_ref[...]
+    for ref in sum_refs:
+        total = total + ref[...].astype(jnp.float32)
+    mlp_out = total.astype(jnp.bfloat16).astype(jnp.float32)
+    normed = layer_norm(mlp_out, gain_ref[...]).astype(jnp.bfloat16)
+    keys = norm_heads(dot(normed, qkv_ref[1]), head_gain_ref[1:2, :])
+    values = dot(normed, qkv_ref[2]).astype(jnp.bfloat16)
+    queries = norm_heads(dot(normed, qkv_ref[0]), head_gain_ref[0:1, :])
+    query_ref[...] = queries
+    view_index = lax.axis_index("view")
+    place = lax.broadcasted_iota(jnp.int32, (tok_view, track_ref.shape[1]), 0)
+    wanted = track_ref[...] - view_index * tok_view
+    chosen = jnp.where(place == wanted, 1.0, 0.0).astype(jnp.bfloat16)
+    picked_ref[...] = lax.dot_general(
+        chosen, queries, (((0,), (0,)), ((), ())), preferred_element_type=jnp.float32
+    ).astype(jnp.bfloat16)
+    asked = track_ref.shape[1] // views
+    half = asked // 2
+    for k in range(views):
+        ref = message_refs[k]
+        start = pl.multiple_of((view_index ^ k) * asked, asked)
+        mine = picked_ref[pl.ds(start, asked), :]
+        ref[:tok_view, :width] = keys
+        ref[:tok_view, width:] = values
+        ref[tok_view:, :width] = mine[:half]
+        ref[tok_view:, width:] = mine[half:]
+
+
+def attend_kernel(counts_ref, query_ref, *refs, views, inner_count):
+    block_refs, refs = refs[:views], refs[views:]
+    depth_ref, track_ref = refs[:2]
+    message_refs, attended_ref, part_ref = (
+        refs[2 : 2 + inner_count],
+        refs[2 + inner_count],
+        refs[3 + inner_count],
+    )
+    tok_view, width = query_ref.shape
+    half = block_refs[0].shape[0] - tok_view
+    view_index = lax.axis_index("view")
+    asked_rows = block_refs[0][tok_view:, :].astype(jnp.float32)
+    for ref in block_refs[1:]:
+        asked_rows = asked_rows + ref[tok_view:, :].astype(jnp.float32)
+    asked_rows = asked_rows.astype(jnp.bfloat16)
+    queries = jnp.concatenate(
+        [query_ref[...], asked_rows[:, :width], asked_rows[:, width:]], axis=0
+    )
+    rows = queries.shape[0]
+    key_place = lax.broadcasted_iota(jnp.int32, (rows, tok_view), 1)
+    valid = [key_place < counts_ref[view_index ^ k] for k in range(views)]
+    lane = lax.broadcasted_iota(jnp.int32, (rows, 128), 1)
+    score_scale = 1.0 / HD**0.5
+    for low in range(0, width, 128):
+        tile = queries[:, low : low + 128]
+        mixed = []
+        for first in range(0, 128, HD):
+            mine = (lane >= first) & (lane < first + HD)
+            head = jnp.where(mine, tile, jnp.zeros_like(tile))
+            scores = []
+            for k, ref in enumerate(block_refs):
+                keys = ref[:tok_view, low : low + 128]
+                score = lax.dot_general(
+                    head, keys, (((1,), (1,)), ((), ())), preferred_element_type=jnp.float32
+                )
+                scores.append(jnp.where(valid[k], score * score_scale, NEG_FILL))
+            row_max = functools.reduce(jnp.maximum, scores).max(axis=1, keepdims=True)
+            weights = [jnp.exp(score - row_max) for score in scores]
+            row_sum = functools.reduce(jnp.add, weights).sum(axis=1, keepdims=True)
+            total = None
+            for k, ref in enumerate(block_refs):
+                values = ref[:tok_view, width + low : width + low + 128]
+                term = dot(weights[k].astype(jnp.bfloat16), values)
+                total = term if total is None else total + term
+            mixed.append((mine, total / row_sum))
+        result = mixed[0][1]
+        for mine, value in mixed[1:]:
+            result = jnp.where(mine, value, result)
+        attended_ref[:, low : low + 128] = result.astype(jnp.bfloat16)
+    depth = dot(attended_ref[:tok_view, :], depth_ref[...]).astype(jnp.bfloat16)
+    part_ref[...] = dot(attended_ref[tok_view:, :], track_ref[...])
+    own = part_ref.shape[0] // inner_count
+    inner_index = lax.axis_index(("branch", "mp"))
+    track_width = part_ref.shape[1]
+    for k, ref in enumerate(message_refs):
+        start = pl.multiple_of((inner_index ^ k) * own, own)
+        ref[:tok_view, :] = depth
+        ref[tok_view:, :track_width] = part_ref[pl.ds(start, own), :].astype(jnp.bfloat16)
+        ref[tok_view:, track_width:] = jnp.zeros(
+            (own, ref.shape[1] - track_width), jnp.bfloat16
+        )
+
+
+def beside(rows):
+    length = rows.shape[0]
+    col = lax.broadcasted_iota(jnp.int32, rows.shape, 0) % GW
+    before = jnp.where(col == 0, 0.0, pltpu.roll(rows, 1, 0))
+    after = jnp.where(col == GW - 1, 0.0, pltpu.roll(rows, length - 1, 0))
+    return jnp.concatenate([before, rows, after], axis=1).astype(jnp.bfloat16)
+
+
+def conv_taps(rows, kernel_ref, bias_ref):
+    wide = beside(rows)
+    out_rows = rows.shape[0] - 2 * GW
+    total = dot(wide[:out_rows], kernel_ref[0])
+    for row_off in range(1, 3):
+        total = total + dot(wide[row_off * GW : row_off * GW + out_rows], kernel_ref[row_off])
+    return total + bias_ref[...]
+
+
+def conv_kernel(counts_ref, *refs, inner_count):
+    message_refs, refs = refs[:inner_count], refs[inner_count:]
+    one_ref, bias_one_ref, two_ref, bias_two_ref, depth_ref, track_ref, feature_ref = refs
+    tok_view = feature_ref.shape[0] - 4 * GW
+    share = depth_ref.shape[0]
+    total = message_refs[0][...].astype(jnp.float32)
+    for ref in message_refs[1:]:
+        total = total + ref[...].astype(jnp.float32)
+    track_ref[...] = total[tok_view:, : track_ref.shape[1]]
+    my_count = counts_ref[lax.axis_index("view")]
+    place = lax.broadcasted_iota(jnp.int32, (tok_view, total.shape[1]), 0)
+    row_valid = jnp.where(place < my_count, 1.0, 0.0)
+    edge = jnp.zeros((2 * GW, total.shape[1]), jnp.float32)
+    feature_ref[: 2 * GW, :] = edge
+    feature_ref[2 * GW + tok_view :, :] = edge
+    features = (total[:tok_view] * row_valid).astype(jnp.bfloat16)
+    feature_ref[2 * GW : 2 * GW + tok_view, :] = features.astype(jnp.float32)
+    begin = lax.axis_index(("branch", "mp")) * share
+    near = share + 4 * GW
+    window = feature_ref[pl.ds(pl.multiple_of(begin, GW), near), :]
+    first = jnp.maximum(conv_taps(window, one_ref, bias_one_ref), 0.0)
+    at = lax.broadcasted_iota(jnp.int32, first.shape, 0) + (begin - GW)
+    first = jnp.where((at >= 0) & (at < tok_view), first, 0.0)
+    first = first.astype(jnp.bfloat16).astype(jnp.float32)
+    depth_ref[...] = conv_taps(first, two_ref, bias_two_ref).astype(depth_ref.dtype)
+
+
+def local_fast(
+    tokens,
+    view_table,
+    view_ids,
+    view_counts,
+    norm_in_gain,
+    in_weight,
+    out_weight,
+    norm_attn_gain,
+    qkv_weight,
+    head_gain,
+    depth_weight,
+    kernel_one,
+    bias_one,
+    kernel_two,
+    bias_two,
+    track_weight,
+    track_ids,
+):
+    shape = jax.ShapeDtypeStruct
+    tok_view, width = tokens.shape
+    views = lax.axis_size("view")
+    branches, cores = lax.axis_size("branch"), lax.axis_size("mp")
+    inner_axes = ("branch", "mp")
+    inner_count = branches * cores
+    head_width = qkv_weight.shape[2]
+    heads_dev = head_width // HD
+    share = tok_view // inner_count
+    hidden_units = in_weight.shape[1]
+    channels = depth_weight.shape[1]
+    opened = run_kernel(open_kernel, shape((8, 128), jnp.float32), [], (), OPEN_GRANT, pl.CostEstimate(flops=1 << 31, bytes_accessed=16 << 20, transcendentals=0))()
+    part, embed = run_kernel(
+        mlp_kernel,
+        [shape((tok_view, width), jnp.bfloat16), shape((1, width), jnp.float32)],
+        [SMEM] + [VMEM] * 6,
+        [pltpu.VMEM((tok_view, hidden_units), jnp.bfloat16)],
+    )(view_ids, view_table, tokens, norm_in_gain.reshape(1, -1), in_weight, out_weight, opened)
+    chip = part.astype(jnp.float32)
+    for got in peers(part, "mp", cores):
+        chip = chip + got.astype(jnp.float32)
+    chip = chip.astype(jnp.bfloat16)
+    sums = [chip] + peers(chip, "branch", branches)
+    asked = track_ids.shape[0] // views
+    message = shape((tok_view + asked // 2, 2 * head_width), jnp.bfloat16)
+    query, *blocks = run_kernel(
+        functools.partial(project_kernel, sums=len(sums), views=views),
+        [shape((tok_view, head_width), jnp.bfloat16)] + [message] * views,
+        [VMEM] * (len(sums) + 6),
+        [pltpu.VMEM((track_ids.shape[0], head_width), jnp.bfloat16)],
+    )(
+        embed,
+        tokens,
+        *sums,
+        norm_attn_gain.reshape(1, -1),
+        qkv_weight.transpose(1, 0, 2),
+        jnp.tile(head_gain, (1, heads_dev)),
+        track_ids.reshape(1, -1),
+    )
+    blocks = blocks[:1] + [
+        lax.ppermute(blocks[k], "view", xor_pairs(views, k)) for k in range(1, views)
+    ]
+    track_width = track_weight.shape[1]
+    own = asked // inner_count
+    message = shape((tok_view + own, channels), jnp.bfloat16)
+    pieces = run_kernel(
+        functools.partial(attend_kernel, views=views, inner_count=inner_count),
+        [message] * inner_count,
+        [SMEM] + [VMEM] * (views + 3),
+        [
+            pltpu.VMEM((tok_view + asked, head_width), jnp.bfloat16),
+            pltpu.VMEM((asked, track_width), jnp.float32),
+        ],
+    )(view_counts, query, *blocks, depth_weight, track_weight)
+    pieces = [pieces[0]] + [
+        lax.ppermute(pieces[k], inner_axes, xor_pairs(inner_count, k))
+        for k in range(1, inner_count)
+    ]
+    return run_kernel(
+        functools.partial(conv_kernel, inner_count=inner_count),
+        [shape((share, channels), jnp.bfloat16), shape((own, track_width), jnp.float32)],
+        [SMEM] + [VMEM] * (inner_count + 4),
+        [pltpu.VMEM((tok_view + 4 * GW, channels), jnp.float32)],
+    )(
+        view_counts,
+        *pieces,
+        kernel_one.reshape(3, 3 * channels, channels),
+        bias_one.reshape(1, -1),
+        kernel_two.reshape(3, 3 * channels, channels),
+        bias_two.reshape(1, -1),
+    )
+
+
+def power_of_two(size):
+    return size & (size - 1) == 0
+
+
+def pick_path(*args):
+    tok_view, head_width = args[0].shape[0], args[8].shape[2]
+    sizes = [lax.axis_size(axis) for axis in ("view", "branch", "mp")]
+    inner_count = sizes[1] * sizes[2]
+    share = tok_view // inner_count
+    fits = all(power_of_two(size) for size in sizes) and share % GW == 0
+    fits = fits and head_width % 128 == 0 and (args[16].shape[0] // sizes[0]) % inner_count == 0
+    return local_fast(*args) if fits else local(*args)
+
+
 def solution(mesh):
     in_specs = (
         P(("groups", "view"), None),
@@ -227,4 +558,4 @@
         P(("groups", "view", "branch", "mp"), None),
         P(("groups", "view", "branch", "mp"), None),
     )
-    return jax.shard_map(local, mesh=mesh, in_specs=in_specs, out_specs=out_specs, check_vma=False)
+    return jax.shard_map(pick_path, mesh=mesh, in_specs=in_specs, out_specs=out_specs, check_vma=False)

time: 206 us -> 43.3 us (0.21)
  waiting for transfers between devices: 119 us -> 22.6 us
  matrix products: 21.9 us -> 0 us
  blocking collectives: 21.9 us -> 0 us
  between operations: 14.7 us -> 0.84 us
  other arithmetic: 9.59 us -> 0.07 us
  Pallas kernels: 0 us -> 7.37 us
  local copies, waits for them, and re-layouts: 8.52 us -> 2.42 us
    unnamed x4 -> x0, waiting for transfers between devices: 80.9 us -> none
    reduce_scatter x2 -> x0, waiting for transfers between devices: 36.7 us -> none  [the longest x1 19.3 us: local(): lax.psum_scatter(jnp.dot(row_block, depth_weight, preferred_element_type=...]
    dot_general x25 -> x0, matrix products: 21.9 us -> none  [the longest x18 11.5 us: conv_rows(): jnp.dot(window, kernel[row_off, col_off], preferred_element_type=jnp.floa...]
    all_gather x2 -> x0, blocking collectives: 21.9 us -> none  [the longest x1 16.1 us: local(): lax.all_gather(stacked, 'view', axis=0, tiled=True)]
    ppermute x4 -> x8, waiting for transfers between devices: 1.41 us -> 22.6 us  [the longest x3 11 us: local_fast(): lax.ppermute(blocks[k], 'view', xor_pairs(views, k))]
    pallas_call x0 -> x5, Pallas kernels: none -> 7.37 us  [the longest x1 2.18 us: local_fast(): run_kernel(functools.partial(attend_kernel, views=views, inner_count=inne...]
    reduce_sum x11 -> x0, other arithmetic: 4.96 us -> none  [the longest x1 1.43 us: local(): my_view = jnp.sum(jnp.where(slot_match, view_ids, 0))]
    unnamed x33 -> x34, local copies, waits for them, and re-layouts: 5.17 us -> 2.34 us
  transfers between devices with their start and end apart: 7 -> 8, of which waited for: 4 -> 6; matrix products, arithmetic and copies ran while one was open for 5% -> 0% of each run, Pallas kernels for 0% -> 0%
where the time goes in v2:
time: 43.3 us; the launch traced here: 43.2 us
  waiting for transfers between devices  22.6 us (52%)
  starting transfers between devices  9.87 us (23%)
  Pallas kernels  7.37 us (17%)
  local copies, waits for them, and re-layouts  2.42 us (6%)
  between operations  0.84 us (2%)
    ppermute x3, waiting for transfers between devices, local_fast(): lax.ppermute(blocks[k], 'view', xor_pairs(views, k))  11 us
    ppermute x2, waiting for transfers between devices, peers(): lax.ppermute(value, axis, xor_pairs(size, k))  7.68 us
    ppermute x3, starting transfers between devices, local_fast(): lax.ppermute(blocks[k], 'view', xor_pairs(views, k))  4.48 us
    ppermute x3, waiting for transfers between devices, local_fast(): lax.ppermute(pieces[k], inner_axes, xor_pairs(inner_count, k))  3.93 us
    ppermute x2, starting transfers between devices, peers(): lax.ppermute(value, axis, xor_pairs(size, k))  3.47 us
    unnamed x34, local copies, waits for them, and re-layouts  2.34 us
    pallas_call x1, Pallas kernels, local_fast(): run_kernel(functools.partial(attend_kernel, views=views, inner_count=inne...  2.18 us
    pallas_call x1, Pallas kernels, local_fast(): run_kernel(functools.partial(conv_kernel, inner_count=inner_count), [shap...  2 us
  transfers between devices with their start and end apart: 8, of which 6 were waited for; matrix products, arithmetic and copies ran while one was open for 0% of the time, Pallas kernels for 0%

profile of v2, /device:TPU:0, one launch (start us, length us, event | category | flops | bytes accessed | tf_op | source)
XLA Modules:
  0.0 43.2 jit_solution(13875868154838103441)
XLA Ops:
  0.6 0.0 copy-start.5
  0.6 0.0 copy-start.1
  0.7 0.0 copy-start
  0.7 0.0 copy-start.9
  0.7 0.0 copy-start.14
  0.7 0.0 copy-start.8
  0.7 0.9 %copy-done.5 = bf16[128,1024]{1,0:T(8,128)(2,1)S(1)} copy-done((bf16[128,1024]{1,0:T(8,128)(2,1)S(1)}, bf16[128,1024]{1,0:T(8,128)(2,1)}, u32[]{:S(2)}) %copy-start.5) | copy-done | bytes 262168
  1.6 0.7 %copy-done.1 = bf16[1024,1024]{1,0:T(8,128)(2,1)S(1)} copy-done((bf16[1024,1024]{1,0:T(8,128)(2,1)S(1)}, bf16[1024,1024]{1,0:T(8,128)(2,1)}, u32[]{:S(2)}) %copy-start.1) | copy-done | bytes 2097176
  2.3 0.6 %copy-done = bf16[1024,1024]{1,0:T(8,128)(2,1)S(1)} copy-done((bf16[1024,1024]{1,0:T(8,128)(2,1)S(1)}, bf16[1024,1024]{1,0:T(8,128)(2,1)}, u32[]{:S(2)}) %copy-start) | copy-done | bytes 2097176
  3.0 0.0 copy-done.9
  3.0 0.0 copy-done.14
  3.0 0.0 copy-done.8
  3.0 0.0 copy-start.16
  3.0 0.0 copy-start.2
  3.0 0.0 copy-start.10
  3.0 0.0 copy-start.15
  3.0 1.6 %shard_map.177 = (bf16[128,1024]{1,0:T(8,128)(2,1)S(1)}, f32[1,1024]{1,0:T(1,128)S(1)}) custom-call(s32[4]{0:T(128)S(1)} %copy-done.14, bf16[4,1024]{1,0:T(4,128)(2,1)S(1)} %copy-done.8, bf16[128,1024]{1,0:T(8,128)(2,1)S(1)} %copy-done.5, f32[1,1024]{1,0:T(1,128)S(1)} %bitcast.11, bf16[1024,1024]{1,0:T(8,128)(2,1)S(1)} %copy-done, ...), custom_call_target="tpu_custom_call" | custom-call | tf_op jit(solution)/shard_map/pallas_call | solution.py:462
  4.6 0.0 copy-start.6
  4.6 0.0 copy-start.7
  4.6 0.0 copy-start.11
  4.6 0.6 %collective-permute-start = (bf16[128,1024]{1,0:T(8,128)(2,1)S(1)}, bf16[128,1024]{1,0:T(8,128)(2,1)S(1)}, u32[]{:S(2)}, u32[]{:S(2)}) collective-permute-start(bf16[128,1024]{1,0:T(8,128)(2,1)S(1)} %get-tuple-element.14), channel_id=1, source_target_pairs={{0,1},{1,0},{2,3},{3,2},{4,5},{5,4},{6,7},{7,6},{8,9},{9,8},{10,11... | collective-permute-start | bytes 786440 | tf_op jit(solution)/shard_map/ppermute | solution.py:238
  5.2 1.2 %collective-permute-done = bf16[128,1024]{1,0:T(8,128)(2,1)S(1)} collective-permute-done((bf16[128,1024]{1,0:T(8,128)(2,1)S(1)}, bf16[128,1024]{1,0:T(8,128)(2,1)S(1)}, u32[]{:S(2)}, u32[]{:S(2)}) %collective-permute-start) | collective-permute-done | bytes 262176 | tf_op jit(solution)/shard_map/ppermute | solution.py:238
  6.3 0.1 add_convert_fusion.refs_0_
  6.4 2.9 %collective-permute-start.1 = (bf16[128,1024]{1,0:T(8,128)(2,1)S(1)}, bf16[128,1024]{1,0:T(8,128)(2,1)S(1)}, u32[]{:S(2)}, u32[]{:S(2)}) collective-permute-start(bf16[128,1024]{1,0:T(8,128)(2,1)S(1)} %add_convert_fusion.refs_0_), channel_id=1, source_target_pairs={{0,2},{2,0},{1,3},{3,1},{4,6},{6,4},{5,7},{7,5},{8,10},{10,8},{9,1... | collective-permute-start | bytes 786440 | tf_op jit(solution)/shard_map/ppermute | solution.py:238
  9.3 0.0 copy-done.16
  9.3 0.1 tile.10.refs_4_
  9.4 6.5 %collective-permute-done.1.refs_1_ = bf16[128,1024]{1,0:T(8,128)(2,1)S(1)} collective-permute-done((bf16[128,1024]{1,0:T(8,128)(2,1)S(1)}, bf16[128,1024]{1,0:T(8,128)(2,1)S(1)}, u32[]{:S(2)}, u32[]{:S(2)}) %collective-permute-start.1) | collective-permute-done | bytes 262176 | tf_op jit(solution)/shard_map/ppermute | solution.py:238
  15.9 0.0 copy-done.2
  15.9 0.0 copy-done.10
  15.9 0.0 copy-done.15
  16.0 0.0 copy-start.3
  16.0 0.0 copy-start.4
  16.0 0.0 copy-start.12
  16.0 0.0 copy-start.13
  16.0 1.6 %shard_map.178 = (bf16[128,256]{1,0:T(8,128)(2,1)S(1)}, bf16[144,512]{1,0:T(8,128)(2,1)S(1)}, bf16[144,512]{1,0:T(8,128)(2,1)S(1)}, bf16[144,512]{1,0:T(8,128)(2,1)S(1)}, bf16[144,512]{1,0:T(8,128)(2,1)S(1)}) custom-call(f32[1,1024]{1,0:T(1,128)S(1)} %get-tuple-element.13.embed_ref, bf16[128,1024]{1,0:T(8,128)(2,1)S(1)} %copy-done.5, ...), custom_call_target="tpu_custom_call" | custom-call | tf_op jit(solution)/shard_map/pallas_call | solution.py:475
  17.6 1.9 %collective-permute-start.2 = (bf16[144,512]{1,0:T(8,128)(2,1)S(1)}, bf16[144,512]{1,0:T(8,128)(2,1)S(1)}, u32[]{:S(2)}, u32[]{:S(2)}) collective-permute-start(bf16[144,512]{1,0:T(8,128)(2,1)S(1)} %get-tuple-element.17), channel_id=1, source_target_pairs={{0,4},{4,0},{8,12},{12,8},{1,5},{5,1},{9,13},{13,9},{2,6},{6,2},{1... | collective-permute-start | bytes 442376 | tf_op jit(solution)/shard_map/ppermute | solution.py:490
  19.5 2.6 %collective-permute-start.3 = (bf16[144,512]{1,0:T(8,128)(2,1)S(1)}, bf16[144,512]{1,0:T(8,128)(2,1)S(1)}, u32[]{:S(2)}, u32[]{:S(2)}) collective-permute-start(bf16[144,512]{1,0:T(8,128)(2,1)S(1)} %get-tuple-element.18), channel_id=1, source_target_pairs={{0,8},{4,12},{8,0},{12,4},{1,9},{5,13},{9,1},{13,5},{2,10},{6,14},... | collective-permute-start | bytes 442376 | tf_op jit(solution)/shard_map/ppermute | solution.py:490
  22.1 0.0 collective-permute-start.4
  22.1 2.7 %collective-permute-done.2.refs_1_ = bf16[144,512]{1,0:T(8,128)(2,1)S(1)} collective-permute-done((bf16[144,512]{1,0:T(8,128)(2,1)S(1)}, bf16[144,512]{1,0:T(8,128)(2,1)S(1)}, u32[]{:S(2)}, u32[]{:S(2)}) %collective-permute-start.2) | collective-permute-done | bytes 147488 | tf_op jit(solution)/shard_map/ppermute | solution.py:490
  24.8 8.3 %collective-permute-done.3.refs_2_ = bf16[144,512]{1,0:T(8,128)(2,1)S(1)} collective-permute-done((bf16[144,512]{1,0:T(8,128)(2,1)S(1)}, bf16[144,512]{1,0:T(8,128)(2,1)S(1)}, u32[]{:S(2)}, u32[]{:S(2)}) %collective-permute-start.3) | collective-permute-done | bytes 147488 | tf_op jit(solution)/shard_map/ppermute | solution.py:490
  33.1 0.0 collective-permute-done.4.refs_3_
  33.1 0.0 copy-done.6
  33.1 0.0 copy-done.7
  33.1 0.0 copy-done.11
  33.1 2.2 %shard_map.179 = (bf16[136,256]{1,0:T(8,128)(2,1)S(1)}, bf16[136,256]{1,0:T(8,128)(2,1)S(1)}, bf16[136,256]{1,0:T(8,128)(2,1)S(1)}, bf16[136,256]{1,0:T(8,128)(2,1)S(1)}) custom-call(s32[4]{0:T(128)S(1)} %copy-done.11, bf16[128,256]{1,0:T(8,128)(2,1)S(1)} %get-tuple-element.15.query_ref, bf16[144,512]{1,0:T(8,128)(2,1)S(1)} %get-tuple-element.16.refs_0_, ...), custom_call_target="tpu_custom_call" | custom-call | tf_op jit(solution)/shard_map/pallas_call | solution.py:495
  35.3 0.1 collective-permute-start.5
  35.4 1.6 %collective-permute-start.6 = (bf16[136,256]{1,0:T(8,128)(2,1)S(1)}, bf16[136,256]{1,0:T(8,128)(2,1)S(1)}, u32[]{:S(2)}, u32[]{:S(2)}) collective-permute-start(bf16[136,256]{1,0:T(8,128)(2,1)S(1)} %get-tuple-element.22), channel_id=1, source_target_pairs={{0,2},{1,3},{2,0},{3,1},{4,6},{5,7},{6,4},{7,5},{8,10},{9,11},{10,... | collective-permute-start | bytes 208904 | tf_op jit(solution)/shard_map/ppermute | solution.py:505
  36.9 0.3 collective-permute-start.7
  37.2 0.0 collective-permute-done.5.refs_1_
  37.2 2.8 %collective-permute-done.6.refs_2_ = bf16[136,256]{1,0:T(8,128)(2,1)S(1)} collective-permute-done((bf16[136,256]{1,0:T(8,128)(2,1)S(1)}, bf16[136,256]{1,0:T(8,128)(2,1)S(1)}, u32[]{:S(2)}, u32[]{:S(2)}) %collective-permute-start.6) | collective-permute-done | bytes 69664 | tf_op jit(solution)/shard_map/ppermute | solution.py:505
  40.0 1.2 %collective-permute-done.7.refs_3_ = bf16[136,256]{1,0:T(8,128)(2,1)S(1)} collective-permute-done((bf16[136,256]{1,0:T(8,128)(2,1)S(1)}, bf16[136,256]{1,0:T(8,128)(2,1)S(1)}, u32[]{:S(2)}, u32[]{:S(2)}) %collective-permute-start.7) | collective-permute-done | bytes 69664 | tf_op jit(solution)/shard_map/ppermute | solution.py:505
  41.2 0.0 copy-done.3
  41.2 0.0 copy-done.4
  41.2 0.0 copy-done.12
  41.2 0.0 copy-done.13
  41.2 2.0 %shard_map.180 = (bf16[32,256]{1,0:T(8,128)(2,1)}, f32[8,128]{1,0:T(8,128)}) custom-call(s32[4]{0:T(128)S(1)} %copy-done.11, bf16[136,256]{1,0:T(8,128)(2,1)S(1)} %get-tuple-element.20.refs_0_, bf16[136,256]{1,0:T(8,128)(2,1)S(1)} %collective-permute-done.5.refs_1_, bf16[136,256]{1,0:T(8,128)(2,1)S(1)} %collective-permute-done.6.refs_2_, ...), custom_call_target="tpu_custom_call" | custom-call | tf_op jit(solution)/shard_map/pallas_call | solution.py:508
  (2 shorter events, 0.0 us)
Async XLA Ops:
  0.6 1.0 %copy-start.5 = (bf16[128,1024]{1,0:T(8,128)(2,1)S(1)}, bf16[128,1024]{1,0:T(8,128)(2,1)}, u32[]{:S(2)}) copy-start(bf16[128,1024]{1,0:T(8,128)(2,1)} %tokens_ref.3) | copy-start | bytes 786436
  0.6 1.7 %copy-start.1 = (bf16[1024,1024]{1,0:T(8,128)(2,1)S(1)}, bf16[1024,1024]{1,0:T(8,128)(2,1)}, u32[]{:S(2)}) copy-start(bf16[1024,1024]{1,0:T(8,128)(2,1)} %out_ref.1) | copy-start | bytes 6291460
  0.7 2.3 %copy-start = (bf16[1024,1024]{1,0:T(8,128)(2,1)S(1)}, bf16[1024,1024]{1,0:T(8,128)(2,1)}, u32[]{:S(2)}) copy-start(bf16[1024,1024]{1,0:T(8,128)(2,1)} %in_ref.1) | copy-start | bytes 6291460
  0.7 2.3 %copy-start.9 = (f32[1024]{0:T(1024)S(1)}, f32[1024]{0:T(1024)}, u32[]{:S(2)}) copy-start(f32[1024]{0:T(1024)} %param.21) | copy-start | bytes 12292
  0.7 2.3 %copy-start.14 = (s32[4]{0:T(128)S(1)}, s32[4]{0:T(128)}, u32[]{:S(2)}) copy-start(s32[4]{0:T(128)} %ids_ref.1) | copy-start | bytes 52
  0.7 2.3 %copy-start.8 = (bf16[4,1024]{1,0:T(4,128)(2,1)S(1)}, bf16[4,1024]{1,0:T(4,128)(2,1)}, u32[]{:S(2)}) copy-start(bf16[4,1024]{1,0:T(4,128)(2,1)} %table_ref.1) | copy-start | bytes 24580
  3.0 6.4 %copy-start.16 = (f32[2,64]{1,0:T(2,128)S(1)}, f32[2,64]{1,0:T(2,128)}, u32[]{:S(2)}) copy-start(f32[2,64]{1,0:T(2,128)} %param.26) | copy-start | bytes 1540
  3.0 13.0 %copy-start.2 = (bf16[1024,3,256]{2,0,1:T(8,128)(2,1)S(1)}, bf16[1024,3,256]{2,0,1:T(8,128)(2,1)}, u32[]{:S(2)}) copy-start(bf16[1024,3,256]{2,0,1:T(8,128)(2,1)} %param.25) | copy-start | bytes 4718596
  3.0 13.0 %copy-start.10 = (f32[1024]{0:T(1024)S(1)}, f32[1024]{0:T(1024)}, u32[]{:S(2)}) copy-start(f32[1024]{0:T(1024)} %param.24) | copy-start | bytes 12292
  3.0 13.0 %copy-start.15 = (s32[128]{0:T(128)S(1)}, s32[128]{0:T(128)}, u32[]{:S(2)}) copy-start(s32[128]{0:T(128)} %param.33) | copy-start | bytes 1540
  4.6 28.5 %copy-start.6 = (bf16[256,256]{1,0:T(8,128)(2,1)S(1)}, bf16[256,256]{1,0:T(8,128)(2,1)}, u32[]{:S(2)}) copy-start(bf16[256,256]{1,0:T(8,128)(2,1)} %refs_4_.1) | copy-start | bytes 393220
  4.6 28.5 %copy-start.7 = (bf16[256,128]{1,0:T(8,128)(2,1)S(1)}, bf16[256,128]{1,0:T(8,128)(2,1)}, u32[]{:S(2)}) copy-start(bf16[256,128]{1,0:T(8,128)(2,1)} %refs_5_.1) | copy-start | bytes 196612
  4.6 28.5 %copy-start.11 = (s32[4]{0:T(128)S(1)}, s32[4]{0:T(128)}, u32[]{:S(2)}) copy-start(s32[4]{0:T(128)} %counts_ref.3) | copy-start | bytes 52
  4.6 1.7 %collective-permute-start = (bf16[128,1024]{1,0:T(8,128)(2,1)S(1)}, bf16[128,1024]{1,0:T(8,128)(2,1)S(1)}, u32[]{:S(2)}, u32[]{:S(2)}) collective-permute-start(bf16[128,1024]{1,0:T(8,128)(2,1)S(1)} %get-tuple-element.14), channel_id=1, source_target_pairs={{0,1},{1,0},{2,3},{3,2},{4,5},{5,4},{6,7},{7,6},{8,9},{9,8},{10,11... | collective-permute-start | bytes 786440 | tf_op jit(solution)/shard_map/ppermute | solution.py:238
  6.4 9.5 %collective-permute-start.1 = (bf16[128,1024]{1,0:T(8,128)(2,1)S(1)}, bf16[128,1024]{1,0:T(8,128)(2,1)S(1)}, u32[]{:S(2)}, u32[]{:S(2)}) collective-permute-start(bf16[128,1024]{1,0:T(8,128)(2,1)S(1)} %add_convert_fusion.refs_0_), channel_id=1, source_target_pairs={{0,2},{2,0},{1,3},{3,1},{4,6},{6,4},{5,7},{7,5},{8,10},{10,8},{9,1... | collective-permute-start | bytes 786440 | tf_op jit(solution)/shard_map/ppermute | solution.py:238
  16.0 25.2 %copy-start.3 = (bf16[3,3,256,256]{3,2,1,0:T(8,128)(2,1)S(1)}, bf16[3,3,256,256]{3,2,1,0:T(8,128)(2,1)}, u32[]{:S(2)}) copy-start(bf16[3,3,256,256]{3,2,1,0:T(8,128)(2,1)} %param.28) | copy-start | bytes 3538948
  16.0 25.2 %copy-start.4 = (bf16[3,3,256,256]{3,2,1,0:T(8,128)(2,1)S(1)}, bf16[3,3,256,256]{3,2,1,0:T(8,128)(2,1)}, u32[]{:S(2)}) copy-start(bf16[3,3,256,256]{3,2,1,0:T(8,128)(2,1)} %param.30) | copy-start | bytes 3538948
  16.0 25.2 %copy-start.12 = (f32[256]{0:T(256)S(1)}, f32[256]{0:T(256)}, u32[]{:S(2)}) copy-start(f32[256]{0:T(256)} %param.29) | copy-start | bytes 3076
  16.0 25.2 %copy-start.13 = (f32[256]{0:T(256)S(1)}, f32[256]{0:T(256)}, u32[]{:S(2)}) copy-start(f32[256]{0:T(256)} %param.31) | copy-start | bytes 3076
  17.6 7.2 %collective-permute-start.2 = (bf16[144,512]{1,0:T(8,128)(2,1)S(1)}, bf16[144,512]{1,0:T(8,128)(2,1)S(1)}, u32[]{:S(2)}, u32[]{:S(2)}) collective-permute-start(bf16[144,512]{1,0:T(8,128)(2,1)S(1)} %get-tuple-element.17), channel_id=1, source_target_pairs={{0,4},{4,0},{8,12},{12,8},{1,5},{5,1},{9,13},{13,9},{2,6},{6,2},{1... | collective-permute-start | bytes 442376 | tf_op jit(solution)/shard_map/ppermute | solution.py:490
  19.5 13.6 %collective-permute-start.3 = (bf16[144,512]{1,0:T(8,128)(2,1)S(1)}, bf16[144,512]{1,0:T(8,128)(2,1)S(1)}, u32[]{:S(2)}, u32[]{:S(2)}) collective-permute-start(bf16[144,512]{1,0:T(8,128)(2,1)S(1)} %get-tuple-element.18), channel_id=1, source_target_pairs={{0,8},{4,12},{8,0},{12,4},{1,9},{5,13},{9,1},{13,5},{2,10},{6,14},... | collective-permute-start | bytes 442376 | tf_op jit(solution)/shard_map/ppermute | solution.py:490
  22.1 11.0 %collective-permute-start.4 = (bf16[144,512]{1,0:T(8,128)(2,1)S(1)}, bf16[144,512]{1,0:T(8,128)(2,1)S(1)}, u32[]{:S(2)}, u32[]{:S(2)}) collective-permute-start(bf16[144,512]{1,0:T(8,128)(2,1)S(1)} %get-tuple-element.19), channel_id=1, source_target_pairs={{0,12},{4,8},{8,4},{12,0},{1,13},{5,9},{9,5},{13,1},{2,14},{6,10},... | collective-permute-start | bytes 442376 | tf_op jit(solution)/shard_map/ppermute | solution.py:490
  35.3 1.9 %collective-permute-start.5 = (bf16[136,256]{1,0:T(8,128)(2,1)S(1)}, bf16[136,256]{1,0:T(8,128)(2,1)S(1)}, u32[]{:S(2)}, u32[]{:S(2)}) collective-permute-start(bf16[136,256]{1,0:T(8,128)(2,1)S(1)} %get-tuple-element.21), channel_id=1, source_target_pairs={{0,1},{1,0},{2,3},{3,2},{4,5},{5,4},{6,7},{7,6},{8,9},{9,8},{10,11... | collective-permute-start | bytes 208904 | tf_op jit(solution)/shard_map/ppermute | solution.py:505
  35.4 4.6 %collective-permute-start.6 = (bf16[136,256]{1,0:T(8,128)(2,1)S(1)}, bf16[136,256]{1,0:T(8,128)(2,1)S(1)}, u32[]{:S(2)}, u32[]{:S(2)}) collective-permute-start(bf16[136,256]{1,0:T(8,128)(2,1)S(1)} %get-tuple-element.22), channel_id=1, source_target_pairs={{0,2},{1,3},{2,0},{3,1},{4,6},{5,7},{6,4},{7,5},{8,10},{9,11},{10,... | collective-permute-start | bytes 208904 | tf_op jit(solution)/shard_map/ppermute | solution.py:505
  36.9 4.2 %collective-permute-start.7 = (bf16[136,256]{1,0:T(8,128)(2,1)S(1)}, bf16[136,256]{1,0:T(8,128)(2,1)S(1)}, u32[]{:S(2)}, u32[]{:S(2)}) collective-permute-start(bf16[136,256]{1,0:T(8,128)(2,1)S(1)} %get-tuple-element.23), channel_id=1, source_target_pairs={{0,3},{1,2},{2,1},{3,0},{4,7},{5,6},{6,5},{7,4},{8,11},{9,10},{10,... | collective-permute-start | bytes 208904 | tf_op jit(solution)/shard_map/ppermute | solution.py:505
